TPU v7x, 512 devices: a whole 4x4x16 slice. The times are simulated.
512 devices in a mesh: grp: 4 (over x_lo, core), dp: 32 (over z, x_hi), mp: 4 (over y).
Axes of the slice: x: 4 (x_hi: 2, x_lo: 2; x = x_hi * 2 + x_lo), y: 4, z: 16, core: 2. Of those that a mesh axis runs over, the one named last changes fastest.
Arguments:
- neighbours: bfloat16 [512, 256, 896], P(('grp', 'dp')), may hold values from -6 to 6
- counts: int32 [512], P(('grp', 'dp')), may hold values from 0 to 2
- owner: int32 [512], P(('grp', 'dp')), may hold values from 0 to 511, as said below
- norm_gain: float32 [896], replicated, may hold values from 0.1 to 1.9
- w_in: bfloat16 [896, 3584], P('dp', 'mp'), may hold values from -0.1875 to 0.1875
- w_out: bfloat16 [3584, 896], P('mp', 'dp'), may hold values from -0.09375 to 0.09375
- w_key: bfloat16 [896, 4096], P('dp', 'mp'), may hold values from -0.1875 to 0.1875
- w_value: bfloat16 [896, 4096], P('dp', 'mp'), may hold values from -0.1875 to 0.1875
- queries: bfloat16 [32768, 4096], P(('grp', 'dp'), 'mp'), may hold values from -150 to 150
Outputs:
- attended: bfloat16 [32768, 4096], P(('grp', 'dp'), 'mp')
Inputs may be any that keep to these rules, and one draw needn't show every extreme that they name: owner is a permutation of the 512 query blocks. Span c stands on device c // 4 of grp+dp (index grp * 32 + dp); block owner[c] lies on device owner[c] // 4, which has the same dp index. Each device keeps 2 of its spans (their blocks lie on the device itself) and sends the other 2 to one other device along grp.
All inputs are finite; a program needn't handle non-finite values.
Results may differ from a plain program's by a relative error of at most 0.02.
Values may be sent and summed in bfloat16 or wider, within the bound.
A program may use at most 64 MiB of HBM per device.

v0:
```python
import jax
import jax.numpy as jnp
from jax import lax
from jax.sharding import PartitionSpec as P

HEAD = 128
NLEN = 128


def place_rows(received, meta, span_count):
    targets = jnp.arange(span_count, dtype=jnp.int32)[:, None]
    picker = meta[:, 0][None, :] == targets
    placed = jnp.einsum(
        "jb,btc->jtc", picker.astype(jnp.bfloat16), received, preferred_element_type=jnp.float32
    ).astype(jnp.bfloat16)
    live_counts = jnp.sum(jnp.where(picker, meta[:, 1][None, :], 0), axis=1).astype(jnp.int32)
    return (placed, live_counts)


def route_table(dest_grp, dest_slot, valid, extra, group_count, capacity):
    entries = dest_grp.shape[0]
    order = jnp.arange(entries, dtype=jnp.int32)
    earlier = (
        valid[None, :]
        & (dest_grp[None, :] == dest_grp[:, None])
        & (order[None, :] < order[:, None])
    )
    rank = jnp.sum(earlier.astype(jnp.int32), axis=1)
    bucket = jnp.where(valid, dest_grp * capacity + rank, -1)
    picker = bucket[None, :] == jnp.arange(group_count * capacity, dtype=jnp.int32)[:, None]
    slot_sent = jnp.sum(jnp.where(picker, dest_slot[None, :] + 1, 0), axis=1) - 1
    extra_sent = jnp.sum(jnp.where(picker, extra[None, :], 0), axis=1)
    meta = jnp.stack([slot_sent, extra_sent], axis=1)
    return (picker, meta)


def bucket_rows(rows, owner, extra, group_count, dp_count):
    span_count = owner.shape[0]
    dest_grp = owner // span_count // dp_count
    dest_slot = owner % span_count
    valid = jnp.ones((span_count,), dtype=bool)
    picker, meta = route_table(dest_grp, dest_slot, valid, extra, group_count, span_count // 2)
    packed = jnp.einsum(
        "bj,jtc->btc", picker.astype(jnp.bfloat16), rows, preferred_element_type=jnp.float32
    ).astype(jnp.bfloat16)
    return (packed, meta)


def attend_local(query_blocks, keys, values, live_counts):
    key_len = keys.shape[1]
    scores = jnp.einsum(
        "cqhd,ckhd->chqk", query_blocks, keys, preferred_element_type=jnp.float32
    ) * HEAD ** (-0.5)
    position = jnp.arange(key_len, dtype=jnp.int32) // NLEN
    live = (position[None, :] < live_counts[:, None])[:, None, None, :]
    masked = jnp.where(live, scores, -1e30)
    top = jnp.maximum(jnp.max(masked, axis=-1), 0.0)
    probs = jnp.where(live, jnp.exp(masked - top[..., None]), 0.0)
    denom = jnp.sum(probs, axis=-1) + jnp.exp(-top)
    weights = probs.astype(jnp.bfloat16)
    mixed = jnp.einsum("chqk,ckhd->cqhd", weights, values, preferred_element_type=jnp.float32)
    mixed = mixed / jnp.transpose(denom, (0, 2, 1))[..., None]
    span_count, span_len = (mixed.shape[0], mixed.shape[1])
    return mixed.astype(jnp.bfloat16).reshape(span_count, span_len, -1)


def on_device(neighbours, counts, owner, norm_gain, w_in, w_out, w_key, w_value, queries):
    span_count, key_len, enc_width = neighbours.shape
    group_count = lax.axis_size("grp")
    dp_count = lax.axis_size("dp")
    local_width = queries.shape[1]
    query_rows = queries.reshape(span_count, -1, local_width)
    flat = neighbours.astype(jnp.float32).reshape(-1, enc_width)
    meansq = jnp.mean(flat * flat, axis=-1, keepdims=True)
    normed = (flat * lax.rsqrt(meansq + 1e-06) * norm_gain).astype(jnp.bfloat16)
    columns = normed
    pre = jnp.dot(
        columns, lax.all_gather(w_in, "dp", axis=0, tiled=True), preferred_element_type=jnp.float32
    )
    hidden = jax.nn.gelu(pre, approximate=False).astype(jnp.bfloat16)
    partial_out = jnp.dot(
        hidden, lax.all_gather(w_out, "dp", axis=1, tiled=True), preferred_element_type=jnp.float32
    )
    total = lax.psum(partial_out, "mp")
    states = (flat + total).astype(jnp.bfloat16).reshape(span_count, key_len, enc_width)
    packed, meta = bucket_rows(states, owner, counts, group_count, dp_count)
    received, received_meta = (
        lax.all_to_all(packed, "grp", split_axis=0, concat_axis=0, tiled=True),
        lax.all_to_all(meta, "grp", split_axis=0, concat_axis=0, tiled=True),
    )
    served, live_counts = place_rows(received, received_meta, span_count)
    served_flat = served.reshape(-1, enc_width)
    columns = served_flat
    key_total = jnp.dot(
        columns, lax.all_gather(w_key, "dp", axis=0, tiled=True), preferred_element_type=jnp.float32
    )
    value_total = jnp.dot(
        columns,
        lax.all_gather(w_value, "dp", axis=0, tiled=True),
        preferred_element_type=jnp.float32,
    )
    heads = w_key.shape[1] // HEAD
    keys = key_total.astype(jnp.bfloat16).reshape(span_count, key_len, heads, HEAD)
    values = value_total.astype(jnp.bfloat16).reshape(span_count, key_len, heads, HEAD)
    query_blocks = query_rows.reshape(span_count, -1, heads, HEAD)
    mixed = attend_local(query_blocks, keys, values, live_counts)
    return mixed.reshape(queries.shape[0], queries.shape[1])


def solution(mesh):
    placed = (
        P(("grp", "dp"), None, None),
        P(("grp", "dp")),
        P(("grp", "dp")),
        P(),
        P("dp", "mp"),
        P("mp", "dp"),
        P("dp", "mp"),
        P("dp", "mp"),
        P(("grp", "dp"), "mp"),
    )
    return jax.shard_map(
        on_device, mesh=mesh, in_specs=placed, out_specs=P(("grp", "dp"), "mp"), check_vma=False
    )
```

profile of v0, /device:TPU:1, one launch (start us, length us, event | category | flops | bytes accessed | tf_op | source)
XLA Modules:
  0.0 737.6 jit_solution(8559613204974902349)
XLA Ops:
  6.5 0.7 all-gather.11.cloned.1.call-update
  7.3 0.7 all-gather.9.cloned.1.call-update
  8.1 1.9 fusion.3
  10.0 2.0 fusion.5
  12.0 142.4 %all-gather.11.cloned.1.call-done = bf16[32,28,896]{2,1,0:T(8,128)(2,1)} async-done(((bf16[1,28,896]{2,1,0:T(8,128)(2,1)}), bf16[32,28,896]{2,1,0:T(8,128)(2,1)}) %all-gather.11.cloned.1.call-update) | async-done | bytes 1605648 | tf_op jit(solution)/shard_map/all_gather | solution.py:82
  154.4 2.4 reshape.107
  156.8 143.2 %all-gather.9.cloned.1.call-done = bf16[32,28,896]{2,1,0:T(8,128)(2,1)} async-done(((bf16[1,28,896]{2,1,0:T(8,128)(2,1)}), bf16[32,28,896]{2,1,0:T(8,128)(2,1)}) %all-gather.9.cloned.1.call-update) | async-done | bytes 1605648 | tf_op jit(solution)/shard_map/all_gather | solution.py:78
  300.0 3.5 reshape.105
  303.5 14.2 %fusion.23 = f32[1024,896]{1,0:T(8,128)} fusion(bf16[896,896]{1,0:T(8,128)(2,1)S(1)} %reshape.107, bf16[1024,896]{1,0:T(8,128)(2,1)S(1)} %fusion.5, bf16[896,896]{1,0:T(8,128)(2,1)} %reshape.105), kind=kOutput, calls=%fused_computation.41 | convolution fusion | flops 3347972096 | bytes 8716288 | tf_op jit(solution)/shard_map/dot_general | solution.py:81
  317.8 0.5 all-gather.13.cloned.1.call-update
  318.4 0.5 all-gather.15.cloned.1.call-update
  319.4 0.6 copy.28
  320.0 13.3 %all-to-all-start = ((s32[4,2,2]{1,2,0:T(2,128)}), s32[4,2,2]{1,2,0:T(2,128)S(1)}, u32[]{:S(2)}, u32[]{:S(2)}) async-start(s32[4,2,2]{1,2,0:T(2,128)} %copy.28), calls=%async_computation | async-start | bytes 8192 | tf_op jit(solution)/shard_map/all_to_all | solution.py:89
  333.4 87.9 %all-reduce.2.cloned.1.call-done = f32[1024,896]{1,0:T(8,128)} async-done(((f32[1024,896]{1,0:T(8,128)}), f32[1024,896]{1,0:T(8,128)}) %all-reduce.2.cloned.1.call-update) | async-done | bytes 3670032 | tf_op jit(solution)/shard_map/psum | solution.py:84
  421.3 2.4 fusion.6
  423.7 2.8 convolution_convert_fusion
  426.4 2.4 copy.31
  428.9 5.7 all-to-all-start.1
  435.0 129.7 %all-gather.13.cloned.1.call-done = bf16[32,28,1024]{2,1,0:T(8,128)(2,1)} async-done(((bf16[1,28,1024]{2,1,0:T(8,128)(2,1)}), bf16[32,28,1024]{2,1,0:T(8,128)(2,1)}) %all-gather.13.cloned.1.call-update) | async-done | bytes 1835024 | tf_op jit(solution)/shard_map/all_gather | solution.py:99
  564.7 2.5 reshape.109
  567.2 144.5 %all-gather.15.cloned.1.call-done = bf16[32,28,1024]{2,1,0:T(8,128)(2,1)} async-done(((bf16[1,28,1024]{2,1,0:T(8,128)(2,1)}), bf16[32,28,1024]{2,1,0:T(8,128)(2,1)}) %all-gather.15.cloned.1.call-update) | async-done | bytes 1835024 | tf_op jit(solution)/shard_map/all_gather | solution.py:95
  711.7 3.7 reshape.111
  715.4 4.5 fusion.25
  720.1 2.4 convert_bitcast_fusion.1
  722.4 0.6 copy.41
  723.1 0.9 copy-done.1
  723.9 2.3 convert_bitcast_fusion
  726.3 0.6 copy.39
  726.9 0.9 bitcast_reduce_fusion
  727.9 0.9 fusion.28
  728.8 1.0 fusion.36
  730.1 0.9 copy.66
  (38 shorter events, 1.6 us)
Async XLA Ops:
  6.5 147.8 %all-gather.11.cloned.1.call-start = ((), (), s32[]{:S(2)}) async-start(), calls=%async_computation.4 | async-start | bytes 1892352 | tf_op jit(solution)/shard_map/all_gather | solution.py:82
  7.3 292.7 %all-gather.9.cloned.1.call-start = ((), (), s32[]{:S(2)}) async-start(), calls=%async_computation.3 | async-start | bytes 1892352 | tf_op jit(solution)/shard_map/all_gather | solution.py:78
  8.0 413.3 %all-reduce.2.cloned.1.call-start = ((), (), s32[]{:S(2)}) async-start(), calls=%async_computation.2 | async-start | bytes 7340032 | tf_op jit(solution)/shard_map/psum | solution.py:84
  317.7 1.2 copy-start.4
  317.7 1.4 copy-start.3
  317.7 103.5 %copy-start = (bf16[4,256,896]{2,1,0:T(8,128)(2,1)S(1)}, bf16[4,256,896]{2,1,0:T(8,128)(2,1)}, u32[]{:S(2)}) copy-start(bf16[4,256,896]{2,1,0:T(8,128)(2,1)} %param.9) | copy-start | bytes 5505028
  317.8 246.9 %all-gather.13.cloned.1.call-start = ((), (), s32[]{:S(2)}) async-start(), calls=%async_computation.5 | async-start | bytes 2162688 | tf_op jit(solution)/shard_map/all_gather | solution.py:99
  318.3 393.3 %all-gather.15.cloned.1.call-start = ((), (), s32[]{:S(2)}) async-start(), calls=%async_computation.6 | async-start | bytes 2162688 | tf_op jit(solution)/shard_map/all_gather | solution.py:95
  320.0 108.9 %all-to-all-start = ((s32[4,2,2]{1,2,0:T(2,128)}), s32[4,2,2]{1,2,0:T(2,128)S(1)}, u32[]{:S(2)}, u32[]{:S(2)}) async-start(s32[4,2,2]{1,2,0:T(2,128)} %copy.28), calls=%async_computation | async-start | bytes 8192 | tf_op jit(solution)/shard_map/all_to_all | solution.py:89
  428.9 5.7 copy-start.2
  428.9 286.5 %all-to-all-start.1 = ((bf16[8,256,896]{2,1,0:T(8,128)(2,1)}), bf16[8,256,896]{2,1,0:T(8,128)(2,1)}, u32[]{:S(2)}, u32[]{:S(2)}) async-start(bf16[8,256,896]{2,1,0:T(8,128)(2,1)} %copy.31), calls=%async_computation.1 | async-start | bytes 7340032 | tf_op jit(solution)/shard_map/all_to_all | solution.py:88
  722.4 1.5 copy-start.1
Sparse Core Ops, SparseCore 0:
  10.4 143.8 all-gather.10
  157.5 142.4 all-gather.8
  317.9 103.3 all-reduce.1
  424.2 140.3 all-gather.12
  567.6 144.0 all-gather.14
where the time goes:
time: 747 us; the launch traced here: 738 us
  waiting for transfers between devices  650 us (87%)
  matrix products  28.1 us (4%)
  starting transfers between devices  19.2 us (3%)
  local copies, waits for them, and re-layouts  19.1 us (3%)
  between operations  13.3 us (2%)
  other arithmetic  7.76 us (1%)
    all_gather x1, waiting for transfers between devices, on_device(): lax.all_gather(w_key, 'dp', axis=0, tiled=True)  145 us
    all_gather x1, waiting for transfers between devices, on_device(): lax.all_gather(w_in, 'dp', axis=0, tiled=True)  143 us
    all_gather x1, waiting for transfers between devices, on_device(): lax.all_gather(w_out, 'dp', axis=1, tiled=True)  142 us
    all_gather x1, waiting for transfers between devices, on_device(): lax.all_gather(w_value, 'dp', axis=0, tiled=True)  130 us
    psum x1, waiting for transfers between devices, on_device(): total = lax.psum(partial_out, 'mp')  87.9 us
    unnamed x19, local copies, waits for them, and re-layouts  15.3 us
  transfers between devices with their start and end apart: 7, of which 5 were waited for; matrix products, arithmetic and copies ran while one was open for 3% of the time, Pallas kernels for 0%

commit v1 on v0

--- a/solution.py
+++ b/solution.py
@@ -1,10 +1,200 @@
+import functools
+
 import jax
 import jax.numpy as jnp
 from jax import lax
+from jax.experimental import pallas as pl
+from jax.experimental.pallas import tpu as pltpu
 from jax.sharding import PartitionSpec as P
 
 HEAD = 128
 NLEN = 128
+MESH = pl.DeviceIdType.MESH
+HALF = 16
+
+
+def ring_place():
+    g, d, m = (lax.axis_index(name) for name in ("grp", "dp", "mp"))
+    core, x, z = g % 2, (d % 2) * 2 + g // 2, d // 2
+    return core, x, z, m
+
+
+def chip_core(x, core, z, m):
+    return ((x % 2) * 2 + core, z * 2 + x // 2, m)
+
+
+class Gather:
+    def __init__(self, zs, own_ref, out_ref, sems):
+        self.zs, self.out = zs, out_ref
+        (self.zsend, self.zrecv, self.fsend, self.frecv, self.one, self.psend, self.precv) = sems
+        self.core, self.x, self.z, self.m = ring_place()
+        turn = 1 - 2 * self.core
+        self.xf, self.xb = (self.x + 4 + turn) % 4, (self.x + 4 - turn) % 4
+        self.xo = (self.x + 2) % 4
+        self.own = own_ref.at[self.x % 2, self.core]
+
+    def partners(self):
+        z, zs = self.z, self.zs
+        return [
+            chip_core(self.x, self.core, (z + 1) % zs, self.m),
+            chip_core(self.x, self.core, (z + zs - 1) % zs, self.m),
+            chip_core(self.xf, self.core, z, self.m),
+            chip_core(self.xb, self.core, z, self.m),
+            chip_core(self.x, 1 - self.core, z, self.m),
+        ]
+
+    def copy(self, src, dst, send, recv, to):
+        return pltpu.make_async_remote_copy(
+            src_ref=src, dst_ref=dst, send_sem=send, recv_sem=recv, device_id=to, device_id_type=MESH
+        )
+
+    def slot(self, x, z):
+        return self.out.at[x, self.core, z]
+
+    def piece(self, x):
+        return self.out.at[x, self.core]
+
+    def ring(self, plus, s):
+        zs = self.zs
+        at = (self.z + zs - s) % zs if plus else (self.z + s) % zs
+        to = self.partners()[0 if plus else 1]
+        src = self.own if s == 0 else self.slot(self.x, at)
+        row = 0 if plus else 1
+        return self.copy(src, self.slot(self.x, at), self.zsend.at[row, s], self.zrecv.at[row, s], to)
+
+    def arrived(self, plus, s):
+        zs = self.zs
+        at = (self.z + zs - s) % zs if plus else (self.z + s) % zs
+        row = 0 if plus else 1
+        ref = self.slot(self.x, at)
+        self.copy(ref, ref, self.zsend.at[row, s - 1], self.zrecv.at[row, s - 1], self.partners()[0]).wait_recv()
+
+    def across(self, at, j, own):
+        src = self.own if own else self.slot(self.x, at)
+        dst = self.slot(self.x, at)
+        to = self.partners()
+        self.copy(src, dst, self.fsend, self.frecv.at[j], to[2]).start()
+        self.copy(src, dst, self.one.at[0], self.one.at[1], to[3]).start()
+
+    def relay(self, at, j):
+        ref = self.slot(self.xb, at)
+        self.copy(ref, ref, self.fsend, self.frecv.at[j], self.partners()[2]).wait_recv()
+        self.copy(ref, ref, self.one.at[2], self.one.at[3], self.partners()[2]).start()
+
+    def fresh(self, s):
+        zs = self.zs
+        if s == 0:
+            return [(self.z, 0)]
+        found = [((self.z + zs - s) % zs, 2 * s - 1)]
+        if s <= (zs - 1) // 2:
+            found.append(((self.z + s) % zs, 2 * s))
+        return found
+
+    def run(self, local):
+        last, back = self.zs // 2, (self.zs - 1) // 2
+        keep = pltpu.make_async_copy(self.own, self.slot(self.x, self.z), local)
+        keep.start()
+        for s in range(last + 1):
+            if s > 0:
+                self.arrived(True, s)
+            if s < last:
+                self.ring(True, s).start()
+            if 0 < s <= back:
+                self.arrived(False, s)
+            if s < back:
+                self.ring(False, s).start()
+            for at, j in self.fresh(s):
+                self.across(at, j, s == 0)
+            if s > 0:
+                for at, j in self.fresh(s - 1):
+                    self.relay(at, j)
+        keep.wait()
+        to = self.partners()[4]
+        swaps = []
+
+        def swap(x):
+            ref = self.piece(x)
+            i = len(swaps)
+            swaps.append(self.copy(ref, ref, self.psend.at[i], self.precv.at[i], to))
+            swaps[-1].start()
+
+        swap(self.x)
+        for at, j in self.fresh(last):
+            self.relay(at, j)
+        swap(self.xb)
+        whole = self.piece(self.xf)
+        self.copy(whole, whole, self.one.at[0], self.one.at[1], to).wait_recv()
+        swap(self.xf)
+        whole = self.piece(self.xo)
+        self.copy(whole, whole, self.one.at[2], self.one.at[3], to).wait_recv()
+        swap(self.xo)
+        for s in range(last):
+            self.ring(True, s).wait_send()
+            if s < back:
+                self.ring(False, s).wait_send()
+        whole = self.piece(self.x)
+        for sem in (self.fsend, self.one.at[0], self.one.at[2]):
+            self.copy(whole, whole, sem, self.one.at[1], to).wait_send()
+        for i, x in enumerate((self.x, self.xb, self.xf, self.xo)):
+            swaps[i].wait_send()
+            ref = self.out.at[x, 1 - self.core]
+            if i in (1, 2):
+                ref = self.out.at[self.xf if i == 1 else self.xb, 1 - self.core]
+            self.copy(ref, ref, self.psend.at[i], self.precv.at[i], to).wait_recv()
+
+
+def gather_sems(zs):
+    return [
+        pltpu.SemaphoreType.DMA((2, zs // 2)),
+        pltpu.SemaphoreType.DMA((2, zs // 2)),
+        pltpu.SemaphoreType.DMA,
+        pltpu.SemaphoreType.DMA((zs,)),
+        pltpu.SemaphoreType.DMA((4,)),
+        pltpu.SemaphoreType.DMA((4,)),
+        pltpu.SemaphoreType.DMA((4,)),
+        pltpu.SemaphoreType.DMA,
+    ]
+
+
+def greet(partners):
+    barrier = pltpu.get_barrier_semaphore()
+    for to in partners:
+        pl.semaphore_signal(barrier, inc=1, device_id=to, device_id_type=MESH)
+    pl.semaphore_wait(barrier, len(partners))
+
+
+def gather_kernel(zs, own_ref, out_ref, *sems):
+    moves = Gather(zs, own_ref, out_ref, sems[:-1])
+    greet(moves.partners())
+    moves.run(sems[-1])
+
+
+def halves(first, second):
+    pair = jnp.stack([first, second])
+    pad = jnp.pad(pair, ((0, 0), (0, 2 * HALF - first.shape[0]), (0, 0)))
+    return pad.reshape(2, 2, HALF, first.shape[1])
+
+
+def whole_pair(out, rows):
+    _, _, zs, _, width = out.shape
+    parts = out.reshape(2, 2, 2, zs, HALF, width)
+    parts = jnp.transpose(parts, (1, 3, 0, 2, 4, 5)).reshape(2, zs * 2, 2 * HALF, width)
+    return [parts[i, :, :rows].reshape(-1, width) for i in range(2)]
+
+
+def gather_pair(first, second, collective_id):
+    rows, width = first.shape
+    zs = lax.axis_size("dp") // 2
+    out = pl.pallas_call(
+        functools.partial(gather_kernel, zs),
+        out_shape=jax.ShapeDtypeStruct((4, 2, zs, HALF, width), first.dtype),
+        in_specs=[pl.BlockSpec(memory_space=pltpu.VMEM)],
+        out_specs=pl.BlockSpec(memory_space=pltpu.VMEM),
+        scratch_shapes=gather_sems(zs),
+        compiler_params=pltpu.CompilerParams(collective_id=collective_id, has_side_effects=True),
+        name=f"gather_pair_{collective_id}",
+    )(halves(first, second))
+    return whole_pair(out, rows)
 
 
 def place_rows(received, meta, span_count):
@@ -73,13 +263,11 @@
     flat = neighbours.astype(jnp.float32).reshape(-1, enc_width)
     meansq = jnp.mean(flat * flat, axis=-1, keepdims=True)
     normed = (flat * lax.rsqrt(meansq + 1e-06) * norm_gain).astype(jnp.bfloat16)
-    columns = normed
-    pre = jnp.dot(
-        columns, lax.all_gather(w_in, "dp", axis=0, tiled=True), preferred_element_type=jnp.float32
-    )
+    full_in, full_out = gather_pair(w_in, w_out.T, 0)
+    pre = jnp.dot(normed, full_in, preferred_element_type=jnp.float32)
     hidden = jax.nn.gelu(pre, approximate=False).astype(jnp.bfloat16)
     partial_out = jnp.dot(
-        hidden, lax.all_gather(w_out, "dp", axis=1, tiled=True), preferred_element_type=jnp.float32
+        hidden, full_out.T, preferred_element_type=jnp.float32
     )
     total = lax.psum(partial_out, "mp")
     states = (flat + total).astype(jnp.bfloat16).reshape(span_count, key_len, enc_width)
@@ -90,15 +278,9 @@
     )
     served, live_counts = place_rows(received, received_meta, span_count)
     served_flat = served.reshape(-1, enc_width)
-    columns = served_flat
-    key_total = jnp.dot(
-        columns, lax.all_gather(w_key, "dp", axis=0, tiled=True), preferred_element_type=jnp.float32
-    )
-    value_total = jnp.dot(
-        columns,
-        lax.all_gather(w_value, "dp", axis=0, tiled=True),
-        preferred_element_type=jnp.float32,
-    )
+    full_key, full_value = gather_pair(w_key, w_value, 1)
+    key_total = jnp.dot(served_flat, full_key, preferred_element_type=jnp.float32)
+    value_total = jnp.dot(served_flat, full_value, preferred_element_type=jnp.float32)
     heads = w_key.shape[1] // HEAD
     keys = key_total.astype(jnp.bfloat16).reshape(span_count, key_len, heads, HEAD)
     values = value_total.astype(jnp.bfloat16).reshape(span_count, key_len, heads, HEAD)

time: 747 us -> 299 us (0.40); the launches traced: 738 us -> 299 us
  waiting for transfers between devices: 650 us -> 88.6 us
  Pallas kernels: 0 us -> 124 us
  starting transfers between devices: 19.2 us -> 9.03 us
  local copies, waits for them, and re-layouts: 19.1 us -> 27.3 us
    all_gather x4 -> x0, waiting for transfers between devices: 560 us -> none  [the longest x1 145 us: on_device(): lax.all_gather(w_key, 'dp', axis=0, tiled=True)]
    pallas_call x0 -> x2, Pallas kernels: none -> 124 us  [gather_pair(): pl.pallas_call(functools.partial(gather_kernel, zs), out_shape=jax.ShapeD...]
    unnamed x19 -> x22, local copies, waits for them, and re-layouts: 15.3 us -> 2.89 us
    another operation x0 -> x4, local copies, waits for them, and re-layouts: none -> 11.4 us  [whole_pair(): return [parts[i, :, :rows].reshape(-1, width) for i in range(2)]]
    all_to_all x1, starting transfers between devices: 13.3 us -> 3.35 us  [on_device(): lax.all_to_all(meta, 'grp', split_axis=0, concat_axis=0, tiled=True)]
  transfers between devices with their start and end apart: 7 -> 3, of which waited for: 5 -> 1; matrix products, arithmetic and copies ran while one was open for 3% -> 6% of each run, Pallas kernels for 0% -> 25%
where the time goes in v1:
time: 299 us
  Pallas kernels  124 us (41%)
  waiting for transfers between devices  88.6 us (30%)
  matrix products  28.2 us (9%)
  local copies, waits for them, and re-layouts  27.3 us (9%)
  between operations  13.6 us (5%)
  starting transfers between devices  9.03 us (3%)
  other arithmetic  8.19 us (3%)
    pallas_call x2, Pallas kernels, gather_pair(): pl.pallas_call(functools.partial(gather_kernel, zs), out_shape=jax.ShapeD...  124 us
    psum x1, waiting for transfers between devices, on_device(): total = lax.psum(partial_out, 'mp')  88.6 us
    dot_general x1, matrix products, on_device(): jnp.dot(hidden, full_out.T, preferred_element_type=jnp.float32)  14.2 us
    another operation x4, local copies, waits for them, and re-layouts, whole_pair(): return [parts[i, :, :rows].reshape(-1, width) for i in range(2)]  11.4 us
  transfers between devices with their start and end apart: 3, of which 1 were waited for; matrix products, arithmetic and copies ran while one was open for 6% of the time, Pallas kernels for 25%

profile of v1, /device:TPU:1, one launch (start us, length us, event | category | flops | bytes accessed | tf_op | source)
XLA Modules:
  0.0 298.6 jit_solution(4764154831331624633)
XLA Ops:
  6.5 1.5 fusion.49
  8.0 47.9 %gather_pair_0.1 = bf16[4,2,16,16,896]{4,3,2,1,0:T(8,128)(2,1)} custom-call(bf16[2,2,16,896]{3,2,1,0:T(8,128)(2,1)} %bitcast.92), custom_call_target="tpu_custom_call" | custom-call | tf_op jit(solution)/shard_map/gather_pair_0/pallas_call | solution.py:188
  56.0 2.6 copy.34
  58.6 2.1 fusion.92
  60.7 2.5 reshape_squeeze.12
  63.2 3.6 %reshape_squeeze.13 = bf16[896,896]{1,0:T(8,128)(2,1)} reshape(bf16[1,32,28,896]{3,2,1,0:T(8,128)(2,1)} %get-tuple-element.10) | data formatting | bytes 3211264 | tf_op jit(solution)/shard_map/reshape;squeeze | solution.py:182
  66.8 0.4 multiply_reduce_fusion
  67.3 1.7 multiply_convert_fusion
  69.0 14.2 %fusion.20 = f32[1024,896]{1,0:T(8,128)} fusion(bf16[896,896]{1,0:T(8,128)(2,1)} %reshape_squeeze.13, bf16[1024,896]{1,0:T(8,128)(2,1)} %bitcast.88, bf16[896,896]{1,0:T(8,128)(2,1)S(1)} %reshape_squeeze.12), kind=kOutput, calls=%fused_computation.38 | convolution fusion | flops 3347972096 | bytes 8716288 | tf_op jit(solution)/shard_map/dot_general | solution.py:269
  83.2 0.6 copy-done.8
  84.3 0.6 copy.32
  84.9 3.3 %all-to-all-start = ((s32[4,2,2]{1,2,0:T(2,128)}), s32[4,2,2]{1,2,0:T(2,128)S(1)}, u32[]{:S(2)}, u32[]{:S(2)}) async-start(s32[4,2,2]{1,2,0:T(2,128)} %copy.32), calls=%async_computation | async-start | bytes 8192 | tf_op jit(solution)/shard_map/all_to_all | solution.py:277
  88.3 88.6 %all-reduce.4.cloned.1.call-done = f32[1024,896]{1,0:T(8,128)} async-done(((f32[1024,896]{1,0:T(8,128)}), f32[1024,896]{1,0:T(8,128)}) %all-reduce.4.cloned.1.call-update) | async-done | bytes 3670032 | tf_op jit(solution)/shard_map/psum | solution.py:272
  176.8 2.4 fusion.3
  179.2 2.8 convolution_convert_fusion
  182.0 2.5 copy.36
  184.6 5.7 %all-to-all-start.1 = ((bf16[8,256,896]{2,1,0:T(8,128)(2,1)}), bf16[8,256,896]{2,1,0:T(8,128)(2,1)}, u32[]{:S(2)}, u32[]{:S(2)}) async-start(bf16[8,256,896]{2,1,0:T(8,128)(2,1)} %copy.36), calls=%async_computation.1 | async-start | bytes 7340032 | tf_op jit(solution)/shard_map/all_to_all | solution.py:276
  190.2 0.7 fusion.48
  190.9 75.8 %gather_pair_1.1 = bf16[4,2,16,16,1024]{4,3,2,1,0:T(8,128)(2,1)} custom-call(bf16[2,2,16,1024]{3,2,1,0:T(8,128)(2,1)} %bitcast.89), custom_call_target="tpu_custom_call" | custom-call | tf_op jit(solution)/shard_map/gather_pair_1/pallas_call | solution.py:188
  266.8 2.6 copy.39
  269.4 1.8 fusion.91
  271.2 3.8 %reshape_squeeze.15 = bf16[896,1024]{1,0:T(8,128)(2,1)} reshape(bf16[1,32,28,1024]{3,2,1,0:T(8,128)(2,1)} %get-tuple-element.7) | data formatting | bytes 3670016 | tf_op jit(solution)/shard_map/reshape;squeeze | solution.py:182
  275.0 1.4 reshape_squeeze.14
  276.8 4.6 %fusion.22 = bf16[4,256,896]{2,0,1:T(4,128)(2,1)S(1)} fusion(bf16[8,256,896]{2,1,0:T(8,128)(2,1)} %all-to-all-done.1, s32[8]{0:T(128)S(1)} %get-tuple-element.12), kind=kOutput, calls=%fused_computation.39 | convolution fusion | flops 15597600 | bytes 5505056 | tf_op jit(solution)/shard_map/jb,btc->jtc/dot_general | solution.py:203
  281.6 2.4 convert_bitcast_fusion
  284.0 0.6 copy.44
  284.6 0.9 bitcast_reduce_fusion
  285.6 0.9 fusion.25
  286.5 2.3 convert_bitcast_fusion.1
  288.9 0.6 copy.46
  289.5 1.0 fusion.33
  290.9 0.9 copy.71
  (41 shorter events, 1.5 us)
Async XLA Ops:
  6.5 170.3 %all-reduce.4.cloned.1.call-start = ((), (), s32[]{:S(2)}) async-start(), calls=%async_computation.2 | async-start | bytes 7340032 | tf_op jit(solution)/shard_map/psum | solution.py:272
  60.7 6.2 %copy-start = (bf16[4,256,896]{2,1,0:T(8,128)(2,1)S(1)}, bf16[4,256,896]{2,1,0:T(8,128)(2,1)}, u32[]{:S(2)}) copy-start(bf16[4,256,896]{2,1,0:T(8,128)(2,1)} %param.9) | copy-start | bytes 5505028
  60.7 6.6 %copy-start.6 = (f32[896]{0:T(1024)S(1)}, f32[896]{0:T(1024)}, u32[]{:S(2)}) copy-start(f32[896]{0:T(1024)} %param.12) | copy-start | bytes 10756
  83.2 0.7 copy-start.8
  83.2 0.9 copy-start.7
  84.9 99.6 %all-to-all-start = ((s32[4,2,2]{1,2,0:T(2,128)}), s32[4,2,2]{1,2,0:T(2,128)S(1)}, u32[]{:S(2)}, u32[]{:S(2)}) async-start(s32[4,2,2]{1,2,0:T(2,128)} %copy.32), calls=%async_computation | async-start | bytes 8192 | tf_op jit(solution)/shard_map/all_to_all | solution.py:277
  184.6 5.7 %copy-start.4 = (bf16[28,1024]{1,0:T(8,128)(2,1)S(1)}, bf16[28,1024]{1,0:T(8,128)(2,1)}, u32[]{:S(2)}) copy-start(bf16[28,1024]{1,0:T(8,128)(2,1)} %param.16) | copy-start | bytes 172036
  184.6 5.7 %copy-start.5 = (bf16[28,1024]{1,0:T(8,128)(2,1)S(1)}, bf16[28,1024]{1,0:T(8,128)(2,1)}, u32[]{:S(2)}) copy-start(bf16[28,1024]{1,0:T(8,128)(2,1)} %param.15) | copy-start | bytes 172036
  184.6 92.2 %all-to-all-start.1 = ((bf16[8,256,896]{2,1,0:T(8,128)(2,1)}), bf16[8,256,896]{2,1,0:T(8,128)(2,1)}, u32[]{:S(2)}, u32[]{:S(2)}) async-start(bf16[8,256,896]{2,1,0:T(8,128)(2,1)} %copy.36), calls=%async_computation.1 | async-start | bytes 7340032 | tf_op jit(solution)/shard_map/all_to_all | solution.py:276
  271.2 3.8 %copy-start.3 = (bf16[256,1024]{1,0:T(8,128)(2,1)S(1)}, bf16[256,1024]{1,0:T(8,128)(2,1)}, u32[]{:S(2)}) copy-start(bf16[256,1024]{1,0:T(8,128)(2,1)} %param.17) | copy-start | bytes 1572868
  276.8 4.8 %copy-start.2 = (bf16[896,1024]{1,0:T(8,128)(2,1)S(1)}, bf16[896,1024]{1,0:T(8,128)(2,1)}, u32[]{:S(2)}) copy-start(bf16[896,1024]{1,0:T(8,128)(2,1)} %reshape_squeeze.15) | copy-start | bytes 5505028
  284.6 1.9 copy-start.1
Sparse Core Ops, SparseCore 0:
  83.3 93.4 all-reduce.3

commit v2 on v1

--- a/solution.py
+++ b/solution.py
@@ -163,10 +163,204 @@
     pl.semaphore_wait(barrier, len(partners))
 
 
-def gather_kernel(zs, own_ref, out_ref, *sems):
-    moves = Gather(zs, own_ref, out_ref, sems[:-1])
-    greet(moves.partners())
+def beside(x):
+    return x + 1 - 2 * (x % 2)
+
+
+def gather_kernel(zs, own_ref, note_ref, out_ref, notes_ref, *sems):
+    moves = Gather(zs, own_ref, out_ref, sems[:-4])
+    core, x, z, m = ring_place()
+    near = [
+        chip_core(x, 1 - core, z, m),
+        chip_core(beside(x), core, z, m),
+        chip_core(beside(x), 1 - core, z, m),
+    ]
+    nsend, nrecv, nlocal = sems[-4:-1]
+    g = lax.axis_index("grp")
+    greet(moves.partners() + near[2:])
+    keep = pltpu.make_async_copy(note_ref, notes_ref.at[g], nlocal)
+    keep.start()
+    told = []
+    for i, to in enumerate(near):
+        told.append(moves.copy(note_ref, notes_ref.at[g], nsend.at[i], nrecv.at[i], to))
+        told[-1].start()
     moves.run(sems[-1])
+    keep.wait()
+    for i, copy in enumerate(told):
+        copy.wait_send()
+        from_core = core if i == 1 else 1 - core
+        from_low = x % 2 if i == 0 else 1 - x % 2
+        ref = notes_ref.at[from_low * 2 + from_core]
+        moves.copy(ref, ref, nsend.at[i], nrecv.at[i], near[i]).wait_recv()
+
+
+class Ring(Gather):
+    def slot(self, x, z):
+        return self.out.at[z]
+
+    def run(self, local, between):
+        last, back = self.zs // 2, (self.zs - 1) // 2
+        keep = pltpu.make_async_copy(self.own, self.slot(self.x, self.z), local)
+        keep.start()
+        for s in range(last + 1):
+            if s > 0:
+                self.arrived(True, s)
+            if s < last:
+                self.ring(True, s).start()
+            if 0 < s <= back:
+                self.arrived(False, s)
+            if s < back:
+                self.ring(False, s).start()
+            if s == last // 2:
+                between()
+        keep.wait()
+        for s in range(last):
+            self.ring(True, s).wait_send()
+            if s < back:
+                self.ring(False, s).wait_send()
+
+
+def sums_kernel(zs, own_ref, part_ref, out_ref, got_ref, relay, ysend, yrecv, zsend, zrecv, local):
+    moves = Ring(zs, own_ref, out_ref, (zsend, zrecv) + (None,) * 5)
+    core, x, z, m = ring_place()
+    up, down, far = (m + 1) % 4, (m + 3) % 4, (m + 2) % 4
+    to_up, to_down = chip_core(x, core, z, up), chip_core(x, core, z, down)
+    greet(moves.partners()[:2] + [to_up, to_down])
+
+    def make(i, src, dst, to):
+        return moves.copy(src, dst, ysend.at[i], yrecv.at[i], to)
+
+    low, high = pl.ds(0, 2), pl.ds(2, 2)
+    copies = [
+        make(0, part_ref.at[low, far], relay.at[0], to_up),
+        make(1, part_ref.at[high, far], relay.at[1], to_down),
+        make(2, part_ref.at[:, up], got_ref.at[0], to_up),
+        make(3, part_ref.at[:, down], got_ref.at[1], to_down),
+        make(4, relay.at[0], got_ref.at[2, low], to_up),
+        make(5, relay.at[1], got_ref.at[2, high], to_down),
+    ]
+    for copy in copies[:4]:
+        copy.start()
+
+    def pass_on():
+        for i in range(2):
+            copies[i].wait_recv()
+            copies[4 + i].start()
+
+    moves.run(local, pass_on)
+    for i, copy in enumerate(copies):
+        copy.wait_send()
+        if i >= 2:
+            copy.wait_recv()
+
+
+def route_kernel(zs, owner_ref, states_ref, piece_ref, full_ref, out_ref, send, cand, rsend, rrecv, ysend, yrecv, xsend, xrecv, psend, precv, local):
+    core, x, z, m = ring_place()
+    g, d = lax.axis_index("grp"), lax.axis_index("dp")
+    turn = 1 - 2 * core
+    xf, xb, xo = (x + 4 + turn) % 4, (x + 4 - turn) % 4, (x + 2) % 4
+    up, down, far = (m + 1) % 4, (m + 3) % 4, (m + 2) % 4
+    to_up, to_down = chip_core(x, core, z, up), chip_core(x, core, z, down)
+    to_f, to_b = chip_core(xf, core, z, m), chip_core(xb, core, z, m)
+    to_core, to_side = chip_core(x, 1 - core, z, m), chip_core(beside(x), core, z, m)
+    spans, block = 4, 4 * lax.axis_size("dp")
+
+    def copy(src, dst, sends, recvs, i, to):
+        return pltpu.make_async_remote_copy(
+            src_ref=src, dst_ref=dst, send_sem=sends.at[i], recv_sem=recvs.at[i], device_id=to, device_id_type=MESH
+        )
+
+    picks = [jnp.int32(0)] * 2
+    finds = [jnp.int32(0)] * spans
+    for source in range(4):
+        low_gap = jnp.where(g // 2 == source // 2, 0, 2)
+        apart = low_gap + jnp.where(core == source % 2, 0, 1)
+        rank = jnp.int32(0)
+        for i in range(spans):
+            target = owner_ref[source * spans + i]
+            leaves = (target < source * block) | (target >= (source + 1) * block)
+            for r in range(2):
+                picks[r] = jnp.where(leaves & (rank == r) & (apart == 0), i, picks[r])
+            spot = jnp.where(apart == 0, i, 4 + 2 * (apart - 1) + jnp.minimum(rank, 1))
+            for j in range(spans):
+                mine = target == (g * lax.axis_size("dp") + d) * spans + j
+                finds[j] = jnp.where(mine, spot, finds[j])
+            rank = rank + jnp.where(leaves, 1, 0)
+
+    for r in range(2):
+        send[r] = states_ref[picks[r]]
+    greet([to_f, to_b, to_core, to_up, to_down])
+    first = [
+        copy(send, cand.at[pl.ds(4, 2)], rsend, rrecv, 0, to_core),
+        copy(send, cand.at[pl.ds(6, 2)], rsend, rrecv, 1, to_side),
+        copy(cand.at[pl.ds(6, 2)], cand.at[pl.ds(8, 2)], rsend, rrecv, 2, to_core),
+    ]
+    first[1].start()
+    first[0].start()
+    held = pltpu.make_async_copy(states_ref, cand.at[pl.ds(0, 4)], local.at[0])
+    held.start()
+    keep = pltpu.make_async_copy(piece_ref, out_ref.at[x, core], local.at[1])
+    keep.start()
+    here = out_ref.at[x, core]
+    back, front, over = out_ref.at[xb, core], out_ref.at[xf, core], out_ref.at[xo, core]
+    to_front = copy(piece_ref, here, xsend, xrecv, 0, to_f)
+    to_back = copy(piece_ref, here, xsend, xrecv, 1, to_b)
+    onward = copy(back, back, xsend, xrecv, 2, to_f)
+    to_front.start()
+    to_back.start()
+    first[1].wait_recv()
+    first[2].start()
+    first[0].wait_recv()
+    held.wait()
+    first[2].wait_recv()
+    for j in range(spans):
+        full_ref[j, m] = cand[finds[j]]
+
+    low, high = pl.ds(0, 2), pl.ds(2, 2)
+
+    def share(i, rows, of, to):
+        ref = full_ref.at[rows, of]
+        return copy(ref, ref, ysend, yrecv, i, to)
+
+    shares = [
+        share(0, low, m, to_up),
+        share(1, high, m, to_down),
+        share(2, high, m, to_up),
+        share(3, low, m, to_down),
+        share(4, low, down, to_up),
+        share(5, high, up, to_down),
+    ]
+    arrivals = [
+        share(0, low, down, to_up),
+        share(1, high, up, to_down),
+        share(2, high, down, to_up),
+        share(3, low, up, to_down),
+        share(4, low, far, to_up),
+        share(5, high, far, to_down),
+    ]
+    for one in shares[:4]:
+        one.start()
+    for i in range(2):
+        arrivals[i].wait_recv()
+        shares[4 + i].start()
+
+    keep.wait()
+    swaps = [copy(ref, ref, psend, precv, i, to_core) for i, ref in enumerate((here, back, front, over))]
+    swaps[0].start()
+    copy(back, back, xsend, xrecv, 0, to_f).wait_recv()
+    onward.start()
+    swaps[1].start()
+    copy(front, front, xsend, xrecv, 1, to_b).wait_recv()
+    swaps[2].start()
+    copy(over, over, xsend, xrecv, 2, to_f).wait_recv()
+    swaps[3].start()
+    for one in arrivals[2:]:
+        one.wait_recv()
+    for one in shares + first + [to_front, to_back, onward] + swaps:
+        one.wait_send()
+    for i, at in enumerate((x, xf, xb, xo)):
+        ref = out_ref.at[at, 1 - core]
+        copy(ref, ref, psend, precv, i, to_core).wait_recv()
 
 
 def halves(first, second):
@@ -182,58 +376,61 @@
     return [parts[i, :, :rows].reshape(-1, width) for i in range(2)]
 
 
-def gather_pair(first, second, collective_id):
+def call(body, ins, outs, scratch, collective_id, name):
+    return pl.pallas_call(
+        body,
+        out_shape=outs,
+        in_specs=[pl.BlockSpec(memory_space=space) for space in ins],
+        out_specs=[pl.BlockSpec(memory_space=pltpu.VMEM)] * len(outs),
+        scratch_shapes=scratch,
+        compiler_params=pltpu.CompilerParams(collective_id=collective_id, has_side_effects=True),
+        name=name,
+    )
+
+
+def dma(*shape):
+    return pltpu.SemaphoreType.DMA(shape)
+
+
+def gather_first(first, second, note):
     rows, width = first.shape
     zs = lax.axis_size("dp") // 2
-    out = pl.pallas_call(
-        functools.partial(gather_kernel, zs),
-        out_shape=jax.ShapeDtypeStruct((4, 2, zs, HALF, width), first.dtype),
-        in_specs=[pl.BlockSpec(memory_space=pltpu.VMEM)],
-        out_specs=pl.BlockSpec(memory_space=pltpu.VMEM),
-        scratch_shapes=gather_sems(zs),
-        compiler_params=pltpu.CompilerParams(collective_id=collective_id, has_side_effects=True),
-        name=f"gather_pair_{collective_id}",
-    )(halves(first, second))
-    return whole_pair(out, rows)
-
-
-def place_rows(received, meta, span_count):
-    targets = jnp.arange(span_count, dtype=jnp.int32)[:, None]
-    picker = meta[:, 0][None, :] == targets
-    placed = jnp.einsum(
-        "jb,btc->jtc", picker.astype(jnp.bfloat16), received, preferred_element_type=jnp.float32
-    ).astype(jnp.bfloat16)
-    live_counts = jnp.sum(jnp.where(picker, meta[:, 1][None, :], 0), axis=1).astype(jnp.int32)
-    return (placed, live_counts)
-
-
-def route_table(dest_grp, dest_slot, valid, extra, group_count, capacity):
-    entries = dest_grp.shape[0]
-    order = jnp.arange(entries, dtype=jnp.int32)
-    earlier = (
-        valid[None, :]
-        & (dest_grp[None, :] == dest_grp[:, None])
-        & (order[None, :] < order[:, None])
-    )
-    rank = jnp.sum(earlier.astype(jnp.int32), axis=1)
-    bucket = jnp.where(valid, dest_grp * capacity + rank, -1)
-    picker = bucket[None, :] == jnp.arange(group_count * capacity, dtype=jnp.int32)[:, None]
-    slot_sent = jnp.sum(jnp.where(picker, dest_slot[None, :] + 1, 0), axis=1) - 1
-    extra_sent = jnp.sum(jnp.where(picker, extra[None, :], 0), axis=1)
-    meta = jnp.stack([slot_sent, extra_sent], axis=1)
-    return (picker, meta)
-
-
-def bucket_rows(rows, owner, extra, group_count, dp_count):
-    span_count = owner.shape[0]
-    dest_grp = owner // span_count // dp_count
-    dest_slot = owner % span_count
-    valid = jnp.ones((span_count,), dtype=bool)
-    picker, meta = route_table(dest_grp, dest_slot, valid, extra, group_count, span_count // 2)
-    packed = jnp.einsum(
-        "bj,jtc->btc", picker.astype(jnp.bfloat16), rows, preferred_element_type=jnp.float32
-    ).astype(jnp.bfloat16)
-    return (packed, meta)
+    outs = [
+        jax.ShapeDtypeStruct((4, 2, zs, HALF, width), first.dtype),
+        jax.ShapeDtypeStruct((4,) + note.shape, note.dtype),
+    ]
+    sems = gather_sems(zs)
+    sems[-1:] = [dma(3), dma(3), pltpu.SemaphoreType.DMA, pltpu.SemaphoreType.DMA]
+    body = functools.partial(gather_kernel, zs)
+    out, notes = call(body, [pltpu.VMEM] * 2, outs, sems, 0, "gather_first")(halves(first, second), note)
+    return whole_pair(out, rows), notes
+
+
+def sum_over_units(parts, key_value):
+    zs = lax.axis_size("dp") // 2
+    spans, _, rows, width = parts.shape
+    outs = [
+        jax.ShapeDtypeStruct((zs,) + key_value.shape[2:], key_value.dtype),
+        jax.ShapeDtypeStruct((3, spans, rows, width), parts.dtype),
+    ]
+    scratch = [pltpu.VMEM((2, 2, rows, width), parts.dtype), dma(6), dma(6)]
+    scratch += [dma(2, zs // 2), dma(2, zs // 2), pltpu.SemaphoreType.DMA]
+    body = functools.partial(sums_kernel, zs)
+    return call(body, [pltpu.VMEM] * 2, outs, scratch, 1, "sum_over_units")(key_value, parts)
+
+
+def route_states(owners, states, piece):
+    zs = piece.shape[0]
+    spans, rows, width = states.shape
+    outs = [
+        jax.ShapeDtypeStruct((spans, 4, rows, width), states.dtype),
+        jax.ShapeDtypeStruct((4, 2) + piece.shape, piece.dtype),
+    ]
+    scratch = [pltpu.VMEM((2, rows, width), states.dtype), pltpu.VMEM((10, rows, width), states.dtype)]
+    scratch += [dma(3), dma(3), dma(6), dma(6), dma(3), dma(3), dma(4), dma(4), dma(2)]
+    body = functools.partial(route_kernel, zs)
+    ins = [pltpu.SMEM, pltpu.VMEM, pltpu.VMEM]
+    return call(body, ins, outs, scratch, 2, "route_states")(owners, states, piece)
 
 
 def attend_local(query_blocks, keys, values, live_counts):
@@ -256,29 +453,32 @@
 
 def on_device(neighbours, counts, owner, norm_gain, w_in, w_out, w_key, w_value, queries):
     span_count, key_len, enc_width = neighbours.shape
-    group_count = lax.axis_size("grp")
-    dp_count = lax.axis_size("dp")
+    dp_count, m = lax.axis_size("dp"), lax.axis_index("mp")
     local_width = queries.shape[1]
     query_rows = queries.reshape(span_count, -1, local_width)
+    note = jnp.pad(jnp.stack([owner, counts]), ((0, 6), (0, 128 - span_count)))
+    (full_in, full_out), notes = gather_first(w_in, w_out.T, note)
     flat = neighbours.astype(jnp.float32).reshape(-1, enc_width)
     meansq = jnp.mean(flat * flat, axis=-1, keepdims=True)
     normed = (flat * lax.rsqrt(meansq + 1e-06) * norm_gain).astype(jnp.bfloat16)
-    full_in, full_out = gather_pair(w_in, w_out.T, 0)
     pre = jnp.dot(normed, full_in, preferred_element_type=jnp.float32)
     hidden = jax.nn.gelu(pre, approximate=False).astype(jnp.bfloat16)
-    partial_out = jnp.dot(
-        hidden, full_out.T, preferred_element_type=jnp.float32
-    )
-    total = lax.psum(partial_out, "mp")
-    states = (flat + total).astype(jnp.bfloat16).reshape(span_count, key_len, enc_width)
-    packed, meta = bucket_rows(states, owner, counts, group_count, dp_count)
-    received, received_meta = (
-        lax.all_to_all(packed, "grp", split_axis=0, concat_axis=0, tiled=True),
-        lax.all_to_all(meta, "grp", split_axis=0, concat_axis=0, tiled=True),
-    )
-    served, live_counts = place_rows(received, received_meta, span_count)
+    partial_out = jnp.dot(hidden, full_out.T, preferred_element_type=jnp.float32)
+    parts = partial_out.astype(jnp.bfloat16).reshape(span_count, 4, key_len // 4, enc_width)
+    piece, got = sum_over_units(parts, halves(w_key, w_value))
+    own = lax.dynamic_index_in_dim(parts, m, 1, keepdims=False).astype(jnp.float32)
+    rows = neighbours.reshape(parts.shape)
+    rows = lax.dynamic_index_in_dim(rows, m, 1, keepdims=False).astype(jnp.float32)
+    got = got.astype(jnp.float32)
+    states = (rows + (own + got[0] + got[1] + got[2])).astype(jnp.bfloat16)
+    owners = notes[:, 0, :span_count].reshape(-1)
+    senders = notes[:, 1, :span_count].reshape(-1)
+    served, pair = route_states(owners, states, piece)
+    full_key, full_value = whole_pair(pair, w_key.shape[0])
+    first_block = (lax.axis_index("grp") * dp_count + lax.axis_index("dp")) * span_count
+    slots = first_block + jnp.arange(span_count, dtype=jnp.int32)
+    live_counts = jnp.sum(jnp.where(owners[None] == slots[:, None], senders[None], 0), axis=1)
     served_flat = served.reshape(-1, enc_width)
-    full_key, full_value = gather_pair(w_key, w_value, 1)
     key_total = jnp.dot(served_flat, full_key, preferred_element_type=jnp.float32)
     value_total = jnp.dot(served_flat, full_value, preferred_element_type=jnp.float32)
     heads = w_key.shape[1] // HEAD

time: 299 us -> 173 us (0.58)
  waiting for transfers between devices: 88.6 us -> 0 us
  between operations: 13.6 us -> 0.21 us
  Pallas kernels: 124 us -> 113 us
  starting transfers between devices: 9.03 us -> 0 us
  matrix products: 28.2 us -> 24.1 us
    psum x1 -> x0, waiting for transfers between devices: 88.6 us -> none  [on_device(): total = lax.psum(partial_out, 'mp')]
    pallas_call x2 -> x3, Pallas kernels: 124 us -> 113 us  [the longest x1 47.9 us: gather_first(): call(body, [pltpu.VMEM] * 2, outs, sems, 0, 'gather_first')]
    all_to_all x2 -> x0, starting transfers between devices: 9.03 us -> none  [the longest x1 5.68 us: on_device(): lax.all_to_all(packed, 'grp', split_axis=0, concat_axis=0, tiled=True)]
    dot_general x2 -> x0, matrix products: 7.39 us -> none  [the longest x1 4.6 us: place_rows(): jnp.einsum('jb,btc->jtc', picker.astype(jnp.bfloat16), received, preferre...]
  transfers between devices with their start and end apart: 3 -> 0, of which waited for: 1 -> 0; matrix products, arithmetic and copies ran while one was open for 6% -> 0% of each run, Pallas kernels for 25% -> 0%
where the time goes in v2:
time: 173 us
  Pallas kernels  113 us (65%)
  local copies, waits for them, and re-layouts  25.1 us (15%)
  matrix products  24.1 us (14%)
  other arithmetic  10.8 us (6%)
    pallas_call x1, Pallas kernels, gather_first(): call(body, [pltpu.VMEM] * 2, outs, sems, 0, 'gather_first')  47.9 us
    pallas_call x1, Pallas kernels, route_states(): call(body, ins, outs, scratch, 2, 'route_states')(owners, states, piece)  35.6 us
    pallas_call x1, Pallas kernels, sum_over_units(): call(body, [pltpu.VMEM] * 2, outs, scratch, 1, 'sum_over_units')  29 us
    dot_general x1, matrix products, on_device(): jnp.dot(hidden, full_out.T, preferred_element_type=jnp.float32)  13.4 us
    another operation x4, local copies, waits for them, and re-layouts, whole_pair(): return [parts[i, :, :rows].reshape(-1, width) for i in range(2)]  9.97 us
    reshape x2, local copies, waits for them, and re-layouts, whole_pair(): parts = out.reshape(2, 2, 2, zs, HALF, width)  5.19 us
    dot_general x1, matrix products, on_device(): jnp.dot(served_flat, full_key, preferred_element_type=jnp.float32)  4.38 us
    dot_general x1, matrix products, on_device(): jnp.dot(served_flat, full_value, preferred_element_type=jnp.float32)  4.38 us

profile of v2, /device:TPU:1, one launch (start us, length us, event | category | flops | bytes accessed | tf_op | source)
XLA Modules:
  0.0 172.7 jit_solution(18374082677762949856)
XLA Ops:
  0.0 1.5 fusion.53
  1.5 0.7 pad_add_fusion
  2.2 0.6 pad.13.note_ref
  2.8 47.9 %gather_first.1 = (bf16[4,2,16,16,896]{4,3,2,1,0:T(8,128)(2,1)}, s32[4,8,128]{2,1,0:T(8,128)}) custom-call(bf16[2,2,16,896]{3,2,1,0:T(8,128)(2,1)} %bitcast.109, s32[8,128]{1,0:T(8,128)} %pad.13.note_ref), custom_call_target="tpu_custom_call" | custom-call | tf_op jit(solution)/shard_map/gather_first/pallas_call | solution.py:405
  50.7 0.8 slice_reduce_fusion
  51.5 0.6 reshape_squeeze.15.owner_ref
  52.2 1.5 fusion.52
  53.7 2.6 %copy.23 = bf16[2,2,2,16,16,896]{5,4,2,0,3,1:T(8,128)(2,1)S(1)} copy(bf16[2,2,2,16,16,896]{5,4,3,2,1,0:T(8,128)(2,1)} %bitcast.99) | data formatting | bytes 7340032 | tf_op jit(solution)/shard_map/reshape | solution.py:374
  56.3 2.1 %fusion.88 = (bf16[1,32,28,896]{3,2,1,0:T(8,128)(2,1)}, bf16[1,32,28,896]{3,2,1,0:T(8,128)(2,1)}) fusion(bf16[2,32,32,896]{3,2,1,0:T(8,128)(2,1)S(1)} %bitcast.96), kind=kLoop, calls=%fused_computation.113 | loop fusion | bytes 6422528 | tf_op jit(solution)/shard_map/slice | solution.py:376
  58.4 2.4 %reshape_squeeze.17 = bf16[896,896]{1,0:T(8,128)(2,1)S(1)} reshape(bf16[1,32,28,896]{3,2,1,0:T(8,128)(2,1)} %get-tuple-element.22) | data formatting | bytes 3211264 | tf_op jit(solution)/shard_map/reshape;squeeze | solution.py:376
  60.8 0.4 fusion
  61.3 1.7 fusion.2
  63.0 2.4 %reshape_squeeze.16 = bf16[896,896]{1,0:T(8,128)(2,1)S(1)} reshape(bf16[1,32,28,896]{3,2,1,0:T(8,128)(2,1)} %get-tuple-element.21) | data formatting | bytes 3211264 | tf_op jit(solution)/shard_map/reshape;squeeze | solution.py:376
  65.4 13.4 %fusion.21 = bf16[1024,896]{1,0:T(8,128)(2,1)} fusion(bf16[896,896]{1,0:T(8,128)(2,1)S(1)} %reshape_squeeze.17, bf16[1024,896]{1,0:T(8,128)(2,1)} %bitcast.105, bf16[896,896]{1,0:T(8,128)(2,1)S(1)} %reshape_squeeze.16), kind=kOutput, calls=%fused_computation.36 | convolution fusion | flops 3348889600 | bytes 6881280 | tf_op jit(solution)/shard_map/dot_general | solution.py:466
  78.8 29.0 %sum_over_units.1 = (bf16[16,16,1024]{2,1,0:T(8,128)(2,1)}, bf16[3,4,64,896]{3,2,1,0:T(8,128)(2,1)}) custom-call(bf16[2,2,16,1024]{3,2,1,0:T(8,128)(2,1)} %bitcast.108, bf16[4,4,64,896]{3,2,1,0:T(8,128)(2,1)} %bitcast.100), custom_call_target="tpu_custom_call" | custom-call | tf_op jit(solution)/shard_map/sum_over_units/pallas_call | solution.py:419
  107.8 1.6 convert_element_type.58
  109.4 2.1 %fusion.44.states_ref = bf16[4,64,896]{2,1,0:T(8,128)(2,1)} fusion(f32[3,4,64,896]{3,2,1,0:T(8,128)S(1)} %convert_element_type.58, bf16[4,4,64,896]{3,2,1,0:T(8,128)(2,1)} %bitcast.101, s32[]{:T(128)S(6)} %select_n.28, bf16[4,4,64,896]{3,2,1,0:T(8,128)(2,1)} %bitcast.97), kind=kLoop, calls=%fused_computation.51 | loop fusion | flops 1605632 | bytes 4128772 | tf_op jit(solution)/shard_map/convert_element_type | solution.py:473
  111.5 35.6 %route_states.1 = (bf16[4,4,64,896]{3,2,1,0:T(8,128)(2,1)}, bf16[4,2,16,16,1024]{4,3,2,1,0:T(8,128)(2,1)}) custom-call(s32[16]{0:T(128)} %reshape_squeeze.15.owner_ref, bf16[4,64,896]{2,1,0:T(8,128)(2,1)} %fusion.44.states_ref, bf16[16,16,1024]{2,1,0:T(8,128)(2,1)} %get-tuple-element.14.piece_ref), custom_call_target="tpu_custom_call" | custom-call | tf_op jit(solution)/shard_map/route_states/pallas_call | solution.py:433
  147.2 2.6 %copy.25 = bf16[2,2,2,16,16,1024]{5,4,2,0,3,1:T(8,128)(2,1)S(1)} copy(bf16[2,2,2,16,16,1024]{5,4,3,2,1,0:T(8,128)(2,1)} %bitcast.98) | data formatting | bytes 8388608 | tf_op jit(solution)/shard_map/reshape | solution.py:374
  149.8 1.8 %fusion.87 = (bf16[1,32,28,1024]{3,2,1,0:T(8,128)(2,1)S(1)}, bf16[1,32,28,1024]{3,2,1,0:T(8,128)(2,1)}) fusion(bf16[2,32,32,1024]{3,2,1,0:T(8,128)(2,1)S(1)} %bitcast.95), kind=kLoop, calls=%fused_computation.112 | loop fusion | bytes 7340032 | tf_op jit(solution)/shard_map/slice | solution.py:376
  151.6 3.7 %reshape_squeeze.18 = bf16[896,1024]{1,0:T(8,128)(2,1)} reshape(bf16[1,32,28,1024]{3,2,1,0:T(8,128)(2,1)} %get-tuple-element.20) | data formatting | bytes 3670016 | tf_op jit(solution)/shard_map/reshape;squeeze | solution.py:376
  155.3 4.4 %convert_bitcast_fusion.1 = bf16[128,8,8,128]{3,1,2,0:T(8,128)(2,1)S(1)} fusion(bf16[1024,896]{1,0:T(8,128)(2,1)} %bitcast.116, bf16[896,1024]{1,0:T(8,128)(2,1)} %reshape_squeeze.18), kind=kOutput, calls=%fused_computation.34 | convolution fusion | flops 1880096768 | bytes 5767168 | tf_op jit(solution)/shard_map/dot_general | solution.py:483
  159.7 2.0 %copy.34 = bf16[128,8,8,128]{3,2,1,0:T(8,128)(2,1)} copy(bf16[128,8,8,128]{3,1,2,0:T(8,128)(2,1)S(1)} %convert_bitcast_fusion.1) | data formatting | bytes 4194304
  161.8 0.2 select_reduce_fusion
  162.1 1.4 reshape_squeeze.19
  163.6 4.4 %convert_bitcast_fusion = bf16[128,8,8,128]{3,1,2,0:T(8,128)(2,1)S(1)} fusion(bf16[1024,896]{1,0:T(8,128)(2,1)} %bitcast.117, bf16[896,1024]{1,0:T(8,128)(2,1)} %reshape_squeeze.19), kind=kOutput, calls=%fused_computation.33 | convolution fusion | flops 1880096768 | bytes 5767168 | tf_op jit(solution)/shard_map/dot_general | solution.py:482
  168.0 0.6 copy.32
  168.6 0.9 bitcast_reduce_fusion
  169.5 0.9 fusion.24
  170.5 1.0 fusion.32
  171.5 0.3 copy.29
  171.8 0.9 copy.53
  (18 shorter events, 0.3 us)
Async XLA Ops:
  56.3 4.5 %copy-start = (bf16[4,256,896]{2,1,0:T(8,128)(2,1)S(1)}, bf16[4,256,896]{2,1,0:T(8,128)(2,1)}, u32[]{:S(2)}) copy-start(bf16[4,256,896]{2,1,0:T(8,128)(2,1)} %param.9) | copy-start | bytes 5505028
  58.4 2.9 %copy-start.4 = (f32[896]{0:T(1024)S(1)}, f32[896]{0:T(1024)}, u32[]{:S(2)}) copy-start(f32[896]{0:T(1024)} %param.12) | copy-start | bytes 10756
  159.7 2.1 %copy-start.3 = (s32[16]{0:T(128)S(1)}, s32[16]{0:T(128)}, u32[]{:S(2)}) copy-start(s32[16]{0:T(128)} %reshape_squeeze.15.owner_ref) | copy-start | bytes 196
  159.7 2.3 %copy-start.2 = (bf16[256,1024]{1,0:T(8,128)(2,1)S(1)}, bf16[256,1024]{1,0:T(8,128)(2,1)}, u32[]{:S(2)}) copy-start(bf16[256,1024]{1,0:T(8,128)(2,1)} %param.17) | copy-start | bytes 1572868
  168.6 1.9 %copy-start.1 = (bf16[128,8,8,128]{3,2,1,0:T(8,128)(2,1)S(1)}, bf16[128,8,8,128]{3,2,1,0:T(8,128)(2,1)}, u32[]{:S(2)}) copy-start(bf16[128,8,8,128]{3,2,1,0:T(8,128)(2,1)} %copy.34) | copy-start | bytes 6291460

commit v3 on v2

v3 whole, which is shorter than its diff:
```python
import functools

import jax
import jax.numpy as jnp
from jax import lax
from jax.experimental import pallas as pl
from jax.experimental.pallas import tpu as pltpu
from jax.sharding import PartitionSpec as P

HEAD = 128
NLEN = 128
MESH = pl.DeviceIdType.MESH
HALF = 16


def ring_place():
    g, d, m = (lax.axis_index(name) for name in ("grp", "dp", "mp"))
    core, x, z = g % 2, (d % 2) * 2 + g // 2, d // 2
    return core, x, z, m


def chip_core(x, core, z, m):
    return ((x % 2) * 2 + core, z * 2 + x // 2, m)


class Gather:
    def __init__(self, zs, own_ref, out_ref, sems):
        self.zs, self.out = zs, out_ref
        (self.zsend, self.zrecv, self.fsend, self.frecv, self.one, self.psend, self.precv) = sems
        self.core, self.x, self.z, self.m = ring_place()
        turn = 1 - 2 * self.core
        self.xf, self.xb = (self.x + 4 + turn) % 4, (self.x + 4 - turn) % 4
        self.xo = (self.x + 2) % 4
        self.own = own_ref.at[self.x % 2, self.core]

    def partners(self):
        z, zs = self.z, self.zs
        return [
            chip_core(self.x, self.core, (z + 1) % zs, self.m),
            chip_core(self.x, self.core, (z + zs - 1) % zs, self.m),
            chip_core(self.xf, self.core, z, self.m),
            chip_core(self.xb, self.core, z, self.m),
            chip_core(self.x, 1 - self.core, z, self.m),
        ]

    def copy(self, src, dst, send, recv, to):
        return pltpu.make_async_remote_copy(
            src_ref=src, dst_ref=dst, send_sem=send, recv_sem=recv, device_id=to, device_id_type=MESH
        )

    def slot(self, x, z):
        return self.out.at[x, self.core, z]

    def piece(self, x):
        return self.out.at[x, self.core]

    def ring(self, plus, s):
        zs = self.zs
        at = (self.z + zs - s) % zs if plus else (self.z + s) % zs
        to = self.partners()[0 if plus else 1]
        src = self.own if s == 0 else self.slot(self.x, at)
        row = 0 if plus else 1
        return self.copy(src, self.slot(self.x, at), self.zsend.at[row, s], self.zrecv.at[row, s], to)

    def arrived(self, plus, s):
        zs = self.zs
        at = (self.z + zs - s) % zs if plus else (self.z + s) % zs
        row = 0 if plus else 1
        ref = self.slot(self.x, at)
        self.copy(ref, ref, self.zsend.at[row, s - 1], self.zrecv.at[row, s - 1], self.partners()[0]).wait_recv()

    def across(self, at, j, own):
        src = self.own if own else self.slot(self.x, at)
        dst = self.slot(self.x, at)
        to = self.partners()
        self.copy(src, dst, self.fsend, self.frecv.at[j], to[2]).start()
        self.copy(src, dst, self.one.at[0], self.one.at[1], to[3]).start()

    def relay(self, at, j):
        ref = self.slot(self.xb, at)
        self.copy(ref, ref, self.fsend, self.frecv.at[j], self.partners()[2]).wait_recv()
        self.copy(ref, ref, self.one.at[2], self.one.at[3], self.partners()[2]).start()

    def fresh(self, s):
        zs = self.zs
        if s == 0:
            return [(self.z, 0)]
        found = [((self.z + zs - s) % zs, 2 * s - 1)]
        if s <= (zs - 1) // 2:
            found.append(((self.z + s) % zs, 2 * s))
        return found

    def run(self, local, also):
        last, back = self.zs // 2, (self.zs - 1) // 2
        keep = pltpu.make_async_copy(self.own, self.slot(self.x, self.z), local)
        keep.start()
        for s in range(last + 1):
            if s > 0:
                self.arrived(True, s)
            if s < last:
                self.ring(True, s).start()
            if 0 < s <= back:
                self.arrived(False, s)
            if s < back:
                self.ring(False, s).start()
            also.step(s)
            for at, j in self.fresh(s):
                self.across(at, j, s == 0)
            if s > 0:
                for at, j in self.fresh(s - 1):
                    self.relay(at, j)
        keep.wait()
        to = self.partners()[4]
        swaps = []

        def swap(x):
            ref = self.piece(x)
            i = len(swaps)
            swaps.append(self.copy(ref, ref, self.psend.at[i], self.precv.at[i], to))
            swaps[-1].start()

        swap(self.x)
        for at, j in self.fresh(last):
            self.relay(at, j)
        swap(self.xb)
        whole = self.piece(self.xf)
        self.copy(whole, whole, self.one.at[0], self.one.at[1], to).wait_recv()
        swap(self.xf)
        whole = self.piece(self.xo)
        self.copy(whole, whole, self.one.at[2], self.one.at[3], to).wait_recv()
        swap(self.xo)
        for s in range(last):
            self.ring(True, s).wait_send()
            if s < back:
                self.ring(False, s).wait_send()
        whole = self.piece(self.x)
        for sem in (self.fsend, self.one.at[0], self.one.at[2]):
            self.copy(whole, whole, sem, self.one.at[1], to).wait_send()
        for i, x in enumerate((self.x, self.xb, self.xf, self.xo)):
            swaps[i].wait_send()
            ref = self.out.at[x, 1 - self.core]
            if i in (1, 2):
                ref = self.out.at[self.xf if i == 1 else self.xb, 1 - self.core]
            self.copy(ref, ref, self.psend.at[i], self.precv.at[i], to).wait_recv()


def gather_sems(zs):
    return [
        pltpu.SemaphoreType.DMA((2, zs // 2)),
        pltpu.SemaphoreType.DMA((2, zs // 2)),
        pltpu.SemaphoreType.DMA,
        pltpu.SemaphoreType.DMA((zs,)),
        pltpu.SemaphoreType.DMA((4,)),
        pltpu.SemaphoreType.DMA((4,)),
        pltpu.SemaphoreType.DMA((4,)),
        pltpu.SemaphoreType.DMA,
    ]


def greet(partners):
    barrier = pltpu.get_barrier_semaphore()
    for to in partners:
        pl.semaphore_signal(barrier, inc=1, device_id=to, device_id_type=MESH)
    pl.semaphore_wait(barrier, len(partners))


def beside(x):
    return x + 1 - 2 * (x % 2)


class Ring(Gather):
    def __init__(self, zs, own_ref, out_ref, sems, local):
        super().__init__(zs, own_ref, out_ref, sems + (None,) * 5)
        self.local = local

    def slot(self, x, z):
        return self.out.at[z]

    def kept(self):
        return pltpu.make_async_copy(self.own, self.slot(self.x, self.z), self.local)

    def step(self, s):
        last, back = self.zs // 2, (self.zs - 1) // 2
        if s > 0:
            self.arrived(True, s)
        if s < last:
            self.ring(True, s).start()
        if 0 < s <= back:
            self.arrived(False, s)
        if s < back:
            self.ring(False, s).start()

    def finish(self):
        self.kept().wait()
        for s in range(self.zs // 2):
            self.ring(True, s).wait_send()
            if s < (self.zs - 1) // 2:
                self.ring(False, s).wait_send()


def unpad(zs, held_ref, full_refs):
    rows = full_refs[0].shape[0] // (2 * zs)
    for a, full in enumerate(full_refs):
        for z in range(zs):
            for high in range(2):
                at = (2 * z + high) * rows
                full[at : at + HALF] = held_ref[high * 2 + a, 0, z]
                full[at + HALF : at + rows] = held_ref[high * 2 + a, 1, z, : rows - HALF]


def gather_kernel(zs, own_ref, later_ref, note_ref, in_ref, out_ref, piece_ref, notes_ref, held, *sems):
    moves = Gather(zs, own_ref, held, sems[:7])
    also = Ring(zs, later_ref, piece_ref, sems[8:10], sems[10])
    nsend, nrecv, nlocal = sems[11:]
    core, x, z, m = ring_place()
    near = [
        chip_core(x, 1 - core, z, m),
        chip_core(beside(x), core, z, m),
        chip_core(beside(x), 1 - core, z, m),
    ]
    g = lax.axis_index("grp")
    greet(moves.partners() + near[2:])
    keep = pltpu.make_async_copy(note_ref, notes_ref.at[g], nlocal)
    keep.start()
    also.kept().start()
    told = []
    for i, to in enumerate(near):
        told.append(moves.copy(note_ref, notes_ref.at[g], nsend.at[i], nrecv.at[i], to))
        told[-1].start()
    moves.run(sems[7], also)
    unpad(zs, held, (in_ref, out_ref))
    also.finish()
    keep.wait()
    for i, copy in enumerate(told):
        copy.wait_send()
        from_core = core if i == 1 else 1 - core
        from_low = x % 2 if i == 0 else 1 - x % 2
        ref = notes_ref.at[from_low * 2 + from_core]
        moves.copy(ref, ref, nsend.at[i], nrecv.at[i], near[i]).wait_recv()


def remote(src, dst, sends, recvs, i, to):
    return pltpu.make_async_remote_copy(
        src_ref=src, dst_ref=dst, send_sem=sends.at[i], recv_sem=recvs.at[i], device_id=to, device_id_type=MESH
    )


def sums_kernel(zs, piece_ref, part_ref, key_ref, value_ref, got_ref, held, relay, ysend, yrecv, xsend, xrecv, psend, precv, local):
    core, x, z, m = ring_place()
    turn = 1 - 2 * core
    xf, xb, xo = (x + 4 + turn) % 4, (x + 4 - turn) % 4, (x + 2) % 4
    up, down, far = (m + 1) % 4, (m + 3) % 4, (m + 2) % 4
    to_up, to_down = chip_core(x, core, z, up), chip_core(x, core, z, down)
    to_f, to_b = chip_core(xf, core, z, m), chip_core(xb, core, z, m)
    to_core = chip_core(x, 1 - core, z, m)
    greet([to_f, to_b, to_core, to_up, to_down])

    def make(i, src, dst, to):
        return remote(src, dst, ysend, yrecv, i, to)

    low, high = pl.ds(0, 2), pl.ds(2, 2)
    copies = [
        make(0, part_ref.at[low, far], relay.at[0], to_up),
        make(1, part_ref.at[high, far], relay.at[1], to_down),
        make(2, part_ref.at[:, up], got_ref.at[0], to_up),
        make(3, part_ref.at[:, down], got_ref.at[1], to_down),
        make(4, relay.at[0], got_ref.at[2, low], to_up),
        make(5, relay.at[1], got_ref.at[2, high], to_down),
    ]
    for copy in copies[:4]:
        copy.start()
    keep = pltpu.make_async_copy(piece_ref, held.at[x, core], local)
    keep.start()
    here = held.at[x, core]
    back, front, over = held.at[xb, core], held.at[xf, core], held.at[xo, core]
    to_front = remote(piece_ref, here, xsend, xrecv, 0, to_f)
    to_back = remote(piece_ref, here, xsend, xrecv, 1, to_b)
    onward = remote(back, back, xsend, xrecv, 2, to_f)
    to_front.start()
    to_back.start()
    swaps = [remote(ref, ref, psend, precv, i, to_core) for i, ref in enumerate((here, back, front, over))]
    keep.wait()
    swaps[0].start()
    for i in range(2):
        copies[i].wait_recv()
        copies[4 + i].start()
    remote(back, back, xsend, xrecv, 0, to_f).wait_recv()
    onward.start()
    swaps[1].start()
    remote(front, front, xsend, xrecv, 1, to_b).wait_recv()
    swaps[2].start()
    remote(over, over, xsend, xrecv, 2, to_f).wait_recv()
    swaps[3].start()
    for i, at in enumerate((x, xf, xb, xo)):
        ref = held.at[at, 1 - core]
        remote(ref, ref, psend, precv, i, to_core).wait_recv()
    unpad(zs, held, (key_ref, value_ref))
    for copy in copies[2:]:
        copy.wait_recv()
    for copy in copies + [to_front, to_back, onward] + swaps:
        copy.wait_send()


def route_kernel(owner_ref, count_ref, states_ref, key_ref, value_ref, query_ref, out_ref, send, cand, full_ref, keys, values, rsend, rrecv, ysend, yrecv, local):
    core, x, z, m = ring_place()
    g, d = lax.axis_index("grp"), lax.axis_index("dp")
    up, down, far = (m + 1) % 4, (m + 3) % 4, (m + 2) % 4
    to_up, to_down = chip_core(x, core, z, up), chip_core(x, core, z, down)
    to_core, to_side = chip_core(x, 1 - core, z, m), chip_core(beside(x), core, z, m)
    spans, block = 4, 4 * lax.axis_size("dp")

    picks = [jnp.int32(0)] * 2
    finds = [jnp.int32(0)] * spans
    lives = [jnp.int32(0)] * spans
    for source in range(4):
        low_gap = jnp.where(g // 2 == source // 2, 0, 2)
        apart = low_gap + jnp.where(core == source % 2, 0, 1)
        rank = jnp.int32(0)
        for i in range(spans):
            target = owner_ref[source * spans + i]
            leaves = (target < source * block) | (target >= (source + 1) * block)
            for r in range(2):
                picks[r] = jnp.where(leaves & (rank == r) & (apart == 0), i, picks[r])
            spot = jnp.where(apart == 0, i, 4 + 2 * (apart - 1) + jnp.minimum(rank, 1))
            for j in range(spans):
                mine = target == (g * lax.axis_size("dp") + d) * spans + j
                finds[j] = jnp.where(mine, spot, finds[j])
                lives[j] = jnp.where(mine, count_ref[source * spans + i], lives[j])
            rank = rank + jnp.where(leaves, 1, 0)

    for r in range(2):
        send[r] = states_ref[picks[r]]
    greet([to_core, to_side, to_up, to_down])
    first = [
        remote(send, cand.at[pl.ds(4, 2)], rsend, rrecv, 0, to_core),
        remote(send, cand.at[pl.ds(6, 2)], rsend, rrecv, 1, to_side),
        remote(cand.at[pl.ds(6, 2)], cand.at[pl.ds(8, 2)], rsend, rrecv, 2, to_core),
    ]
    first[1].start()
    first[0].start()
    held = pltpu.make_async_copy(states_ref, cand.at[pl.ds(0, 4)], local)
    held.start()
    first[1].wait_recv()
    first[2].start()
    first[0].wait_recv()
    held.wait()
    first[2].wait_recv()
    for j in range(spans):
        full_ref[j, m] = cand[finds[j]]

    low, high = pl.ds(0, 2), pl.ds(2, 2)

    def share(i, rows, of, to):
        ref = full_ref.at[rows, of]
        return remote(ref, ref, ysend, yrecv, i, to)

    shares = [
        share(0, low, m, to_up),
        share(1, high, m, to_down),
        share(2, high, m, to_up),
        share(3, low, m, to_down),
        share(4, low, down, to_up),
        share(5, high, up, to_down),
    ]
    arrivals = [
        share(0, low, down, to_up),
        share(1, high, up, to_down),
        share(2, high, down, to_up),
        share(3, low, up, to_down),
        share(4, low, far, to_up),
        share(5, high, far, to_down),
    ]
    for one in shares[:4]:
        one.start()
    project = functools.partial(project_rows, full_ref, ((key_ref, keys), (value_ref, values)))
    for i in range(2):
        arrivals[i].wait_recv()
        shares[4 + i].start()
    project(m)
    arrivals[2].wait_recv()
    project(down)
    arrivals[3].wait_recv()
    project(up)
    arrivals[4].wait_recv()
    arrivals[5].wait_recv()
    project(far)
    attend(query_ref, keys, values, lives, out_ref)
    for one in shares + first:
        one.wait_send()


def project_rows(full_ref, pairs, of):
    spans, _, rows, width = full_ref.shape
    block = full_ref[:, of].reshape(spans * rows, width)
    tile = min(256, pairs[0][0].shape[1])
    for weight, result in pairs:

        def column(t, carry, weight=weight, result=result):
            at = pl.ds(pl.multiple_of(t * tile, tile), tile)
            made = jnp.dot(block, weight[:, at], preferred_element_type=jnp.float32)
            result[:, of, :, at] = made.astype(result.dtype).reshape(spans, rows, tile)
            return carry

        lax.fori_loop(0, weight.shape[1] // tile, column, 0)


def attend(query_ref, keys, values, lives, out_ref):
    spans, quarters, rows, width = keys.shape
    length = quarters * rows
    lines = query_ref.shape[0] // spans
    position = lax.broadcasted_iota(jnp.int32, (lines, length), 1)

    def head(h, carry):
        at = pl.ds(pl.multiple_of(h * HEAD, HEAD), HEAD)
        for j in range(spans):
            of = pl.ds(j * lines, lines)
            key = keys[j, :, :, at].reshape(length, HEAD)
            value = values[j, :, :, at].reshape(length, HEAD)
            scores = lax.dot_general(
                query_ref[of, at], key, (((1,), (1,)), ((), ())), preferred_element_type=jnp.float32
            ) * HEAD ** (-0.5)
            live = position < lives[j] * NLEN
            masked = jnp.where(live, scores, -1e30)
            top = jnp.maximum(jnp.max(masked, axis=-1, keepdims=True), 0.0)
            probs = jnp.where(live, jnp.exp(masked - top), 0.0)
            denom = jnp.sum(probs, axis=-1, keepdims=True) + jnp.exp(-top)
            mixed = jnp.dot(probs.astype(jnp.bfloat16), value, preferred_element_type=jnp.float32)
            out_ref[of, at] = (mixed / denom).astype(out_ref.dtype)
        return carry

    lax.fori_loop(0, width // HEAD, head, 0)


def halves(first, second):
    pair = jnp.stack([first, second])
    pad = jnp.pad(pair, ((0, 0), (0, 2 * HALF - first.shape[0]), (0, 0)))
    return pad.reshape(2, 2, HALF, first.shape[1])


def call(body, ins, outs, scratch, collective_id, name):
    return pl.pallas_call(
        body,
        out_shape=outs,
        in_specs=[pl.BlockSpec(memory_space=space) for space in ins],
        out_specs=[pl.BlockSpec(memory_space=pltpu.VMEM)] * len(outs),
        scratch_shapes=scratch,
        compiler_params=pltpu.CompilerParams(collective_id=collective_id, has_side_effects=True),
        name=name,
    )


def dma(*shape):
    return pltpu.SemaphoreType.DMA(shape)


def gather_first(first, second, later, note):
    rows, width = first.shape
    zs = lax.axis_size("dp") // 2
    whole = jax.ShapeDtypeStruct((rows * zs * 2, width), first.dtype)
    outs = [
        whole,
        whole,
        jax.ShapeDtypeStruct((zs,) + later.shape[2:], later.dtype),
        jax.ShapeDtypeStruct((4,) + note.shape, note.dtype),
    ]
    one = pltpu.SemaphoreType.DMA
    scratch = [pltpu.VMEM((4, 2, zs, HALF, width), first.dtype)] + gather_sems(zs)
    scratch += [dma(2, zs // 2), dma(2, zs // 2), one, dma(3), dma(3), one]
    body = functools.partial(gather_kernel, zs)
    return call(body, [pltpu.VMEM] * 3, outs, scratch, 0, "gather_first")(halves(first, second), later, note)


def sum_over_units(parts, piece, features):
    zs = piece.shape[0]
    spans, _, rows, width = parts.shape
    whole = jax.ShapeDtypeStruct((features, piece.shape[2]), piece.dtype)
    outs = [whole, whole, jax.ShapeDtypeStruct((3, spans, rows, width), parts.dtype)]
    scratch = [pltpu.VMEM((4, 2) + piece.shape, piece.dtype), pltpu.VMEM((2, 2, rows, width), parts.dtype)]
    scratch += [dma(6), dma(6), dma(3), dma(3), dma(4), dma(4), pltpu.SemaphoreType.DMA]
    body = functools.partial(sums_kernel, zs)
    return call(body, [pltpu.VMEM] * 2, outs, scratch, 1, "sum_over_units")(piece, parts)


def route_and_attend(owners, senders, states, key, value, queries):
    spans, rows, width = states.shape
    kind = states.dtype
    outs = [jax.ShapeDtypeStruct(queries.shape, kind)]
    held = pltpu.VMEM((spans, 4, rows, key.shape[1]), kind)
    scratch = [
        pltpu.VMEM((2, rows, width), kind),
        pltpu.VMEM((10, rows, width), kind),
        pltpu.VMEM((spans, 4, rows, width), kind),
        held,
        held,
    ]
    scratch += [dma(3), dma(3), dma(6), dma(6), pltpu.SemaphoreType.DMA]
    ins = [pltpu.SMEM] * 2 + [pltpu.VMEM] * 4
    return call(route_kernel, ins, outs, scratch, 2, "route_and_attend")(owners, senders, states, key, value, queries)[0]


def on_device(neighbours, counts, owner, norm_gain, w_in, w_out, w_key, w_value, queries):
    span_count, key_len, enc_width = neighbours.shape
    m = lax.axis_index("mp")
    note = jnp.pad(jnp.stack([owner, counts]), ((0, 6), (0, 128 - span_count)))
    full_in, full_out, piece, notes = gather_first(w_in, w_out.T, halves(w_key, w_value), note)
    flat = neighbours.astype(jnp.float32).reshape(-1, enc_width)
    meansq = jnp.mean(flat * flat, axis=-1, keepdims=True)
    normed = (flat * lax.rsqrt(meansq + 1e-06) * norm_gain).astype(jnp.bfloat16)
    pre = jnp.dot(normed, full_in, preferred_element_type=jnp.float32)
    hidden = jax.nn.gelu(pre, approximate=False).astype(jnp.bfloat16)
    partial_out = jnp.dot(hidden, full_out.T, preferred_element_type=jnp.float32)
    parts = partial_out.astype(jnp.bfloat16).reshape(span_count, 4, key_len // 4, enc_width)
    full_key, full_value, got = sum_over_units(parts, piece, enc_width)
    own = lax.dynamic_index_in_dim(parts, m, 1, keepdims=False).astype(jnp.float32)
    rows = neighbours.reshape(parts.shape)
    rows = lax.dynamic_index_in_dim(rows, m, 1, keepdims=False).astype(jnp.float32)
    got = got.astype(jnp.float32)
    states = (rows + (own + got[0] + got[1] + got[2])).astype(jnp.bfloat16)
    owners = notes[:, 0, :span_count].reshape(-1)
    senders = notes[:, 1, :span_count].reshape(-1)
    return route_and_attend(owners, senders, states, full_key, full_value, queries)


def solution(mesh):
    placed = (
        P(("grp", "dp"), None, None),
        P(("grp", "dp")),
        P(("grp", "dp")),
        P(),
        P("dp", "mp"),
        P("mp", "dp"),
        P("dp", "mp"),
        P("dp", "mp"),
        P(("grp", "dp"), "mp"),
    )
    return jax.shard_map(
        on_device, mesh=mesh, in_specs=placed, out_specs=P(("grp", "dp"), "mp"), check_vma=False
    )
```

time: 173 us -> 155 us (0.90)
  local copies, waits for them, and re-layouts: 25.1 us -> 4.58 us
  Pallas kernels: 113 us -> 124 us
  matrix products: 24.1 us -> 13.9 us
    dot_general x4 -> x0, matrix products: 10.7 us -> none  [the longest x1 4.38 us: on_device(): jnp.dot(served_flat, full_key, preferred_element_type=jnp.float32)]
    another operation x4 -> x1, local copies, waits for them, and re-layouts: 9.97 us -> 0.62 us  [on_device(): senders = notes[:, 1, :span_count].reshape(-1)]
    pallas_call x2, Pallas kernels: 83.5 us -> 91.5 us  [the longest x1 50.4 us: gather_first(): call(body, [pltpu.VMEM] * 3, outs, scratch, 0, 'gather_first')]
    reshape x2 -> x0, local copies, waits for them, and re-layouts: 5.19 us -> none  [whole_pair(): parts = out.reshape(2, 2, 2, zs, HALF, width)]
    slice x2 -> x0, local copies, waits for them, and re-layouts: 3.88 us -> none  [whole_pair(): return [parts[i, :, :rows].reshape(-1, width) for i in range(2)]]
    pallas_call x1, Pallas kernels: 29 us -> 32.4 us  [sum_over_units(): call(body, [pltpu.VMEM] * 2, outs, scratch, 1, 'sum_over_units')]
    unnamed x14 -> x6, local copies, waits for them, and re-layouts: 3.61 us -> 1.88 us
where the time goes in v3:
time: 155 us
  Pallas kernels  124 us (80%)
  matrix products  13.9 us (9%)
  other arithmetic  12.1 us (8%)
  local copies, waits for them, and re-layouts  4.58 us (3%)
    pallas_call x1, Pallas kernels, gather_first(): call(body, [pltpu.VMEM] * 3, outs, scratch, 0, 'gather_first')  50.4 us
    pallas_call x1, Pallas kernels, route_and_attend(): call(route_kernel, ins, outs, scratch, 2, 'route_and_attend')  41.2 us
    pallas_call x1, Pallas kernels, sum_over_units(): call(body, [pltpu.VMEM] * 2, outs, scratch, 1, 'sum_over_units')  32.4 us
    dot_general x1, matrix products, on_device(): jnp.dot(hidden, full_out.T, preferred_element_type=jnp.float32)  13.9 us
    another operation x2, other arithmetic, halves(): pair = jnp.stack([first, second])  3.18 us

profile of v3, /device:TPU:1, one launch (start us, length us, event | category | flops | bytes accessed | tf_op | source)
XLA Modules:
  0.0 154.6 jit_solution(11460467863264804759)
XLA Ops:
  0.0 0.0 copy-start
  0.0 1.6 %fusion.27 = bf16[2,32,896]{2,1,0:T(8,128)(2,1)} fusion(bf16[1,28,896]{2,1,0:T(8,128)(2,1)} %bitcast.61, bf16[1,28,896]{2,1,0:T(8,128)(2,1)} %bitcast.62), kind=kLoop, calls=%fused_computation.40 | loop fusion | flops 401408 | bytes 215040 | tf_op jit(solution)/shard_map/stack | solution.py:435
  1.6 1.5 fusion.26
  3.2 0.7 pad_add_fusion
  3.9 0.6 pad.14.note_ref
  4.5 50.4 %gather_first.1 = (bf16[896,896]{1,0:T(8,128)(2,1)}, bf16[896,896]{1,0:T(8,128)(2,1)}, bf16[16,16,1024]{2,1,0:T(8,128)(2,1)}, s32[4,8,128]{2,1,0:T(8,128)}) custom-call(bf16[2,2,16,896]{3,2,1,0:T(8,128)(2,1)} %bitcast.58, bf16[2,2,16,1024]{3,2,1,0:T(8,128)(2,1)} %bitcast.57, s32[8,128]{1,0:T(8,128)} %pad.14.note_ref), custom_call_target="tpu_custom_call" | custom-call | tf_op jit(solution)/shard_map/gather_first/pallas_call | solution.py:470
  54.8 0.8 slice_reduce_fusion
  55.6 0.7 reshape_squeeze.6.owner_ref
  56.3 0.6 reshape_squeeze.7.count_ref
  56.9 0.0 copy-start.1
  56.9 2.1 %multiply_reduce_fusion = f32[4,256]{1,0:T(4,128)S(1)} fusion(bf16[4,256,896]{2,1,0:T(8,128)(2,1)} %param.9), kind=kLoop, calls=%fused_computation.20 | loop fusion | flops 2751488 | bytes 1839104 | tf_op jit(solution)/shard_map/reduce_sum | solution.py:507
  59.0 0.0 copy-done
  59.0 2.4 %fusion.4 = bf16[1024,896]{1,0:T(8,128)(2,1)} fusion(f32[896]{0:T(1024)} %param.12, f32[1024]{0:T(1024)S(1)} %bitcast.63, bf16[4,256,896]{2,1,0:T(8,128)(2,1)S(1)} %copy-done), kind=kLoop, calls=%fused_computation.6 | loop fusion | flops 3670016 | bytes 3677696 | tf_op jit(solution)/shard_map/convert_element_type | solution.py:508
  61.4 0.0 copy-done.1
  61.4 13.9 %fusion.14 = bf16[1024,896]{1,0:T(8,128)(2,1)} fusion(bf16[896,896]{1,0:T(8,128)(2,1)} %get-tuple-element.14, bf16[1024,896]{1,0:T(8,128)(2,1)} %fusion.4, bf16[896,896]{1,0:T(8,128)(2,1)S(1)} %copy-done.1), kind=kOutput, calls=%fused_computation.24 | convolution fusion | flops 3348889600 | bytes 6881280 | tf_op jit(solution)/shard_map/dot_general | solution.py:511
  75.3 32.4 %sum_over_units.1 = (bf16[896,1024]{1,0:T(8,128)(2,1)}, bf16[896,1024]{1,0:T(8,128)(2,1)}, bf16[3,4,64,896]{3,2,1,0:T(8,128)(2,1)}) custom-call(bf16[16,16,1024]{2,1,0:T(8,128)(2,1)} %get-tuple-element.15.piece_ref, bf16[4,4,64,896]{3,2,1,0:T(8,128)(2,1)} %bitcast.55), custom_call_target="tpu_custom_call" | custom-call | tf_op jit(solution)/shard_map/sum_over_units/pallas_call | solution.py:481
  107.8 1.6 %convert_element_type.42 = f32[3,4,64,896]{3,2,1,0:T(8,128)S(1)} convert(bf16[3,4,64,896]{3,2,1,0:T(8,128)(2,1)} %get-tuple-element.16) | non-fusion elementwise | flops 688128 | bytes 4128768 | tf_op jit(solution)/shard_map/convert_element_type | solution.py:517
  109.4 2.1 %fusion.19.states_ref = bf16[4,64,896]{2,1,0:T(8,128)(2,1)} fusion(f32[3,4,64,896]{3,2,1,0:T(8,128)S(1)} %convert_element_type.42, bf16[4,4,64,896]{3,2,1,0:T(8,128)(2,1)} %bitcast.56, s32[]{:T(128)S(6)} %select_n.5, bf16[4,4,64,896]{3,2,1,0:T(8,128)(2,1)} %bitcast.54), kind=kLoop, calls=%fused_computation.28 | loop fusion | flops 1605632 | bytes 4128772 | tf_op jit(solution)/shard_map/convert_element_type | solution.py:518
  111.5 41.2 %route_and_attend.1 = bf16[256,1024]{1,0:T(8,128)(2,1)} custom-call(s32[16]{0:T(128)} %reshape_squeeze.6.owner_ref, s32[16]{0:T(128)} %reshape_squeeze.7.count_ref, bf16[4,64,896]{2,1,0:T(8,128)(2,1)} %fusion.19.states_ref, bf16[896,1024]{1,0:T(8,128)(2,1)} %get-tuple-element.17.key_ref, bf16[896,1024]{1,0:T(8,128)(2,1)} %get-tuple-element.18.value_ref, ...), custom_call_target="tpu_custom_call" | custom-call | tf_op jit(solution)/shard_map/route_and_attend/pallas_call | solution.py:498
  152.7 1.9 %copy.17 = bf16[256,1024]{1,0:T(8,128)(2,1)} copy(bf16[256,1024]{1,0:T(8,128)(2,1)} %route_and_attend.1) | data formatting | bytes 1048576
  (2 shorter events, 0.0 us)
Async XLA Ops:
  0.0 59.0 %copy-start = (bf16[4,256,896]{2,1,0:T(8,128)(2,1)S(1)}, bf16[4,256,896]{2,1,0:T(8,128)(2,1)}, u32[]{:S(2)}) copy-start(bf16[4,256,896]{2,1,0:T(8,128)(2,1)} %param.9) | copy-start | bytes 5505028
  56.9 4.5 %copy-start.1 = (bf16[896,896]{1,0:T(8,128)(2,1)S(1)}, bf16[896,896]{1,0:T(8,128)(2,1)}, u32[]{:S(2)}) copy-start(bf16[896,896]{1,0:T(8,128)(2,1)} %get-tuple-element.13) | copy-start | bytes 4816900

commit v4 on v3

--- a/solution.py
+++ b/solution.py
@@ -90,7 +90,7 @@
             found.append(((self.z + s) % zs, 2 * s))
         return found
 
-    def run(self, local, also):
+    def run(self, local, also, work):
         last, back = self.zs // 2, (self.zs - 1) // 2
         keep = pltpu.make_async_copy(self.own, self.slot(self.x, self.z), local)
         keep.start()
@@ -106,6 +106,8 @@
             also.step(s)
             for at, j in self.fresh(s):
                 self.across(at, j, s == 0)
+            if s < last:
+                work(s)
             if s > 0:
                 for at, j in self.fresh(s - 1):
                     self.relay(at, j)
@@ -208,7 +210,17 @@
                 full[at + HALF : at + rows] = held_ref[high * 2 + a, 1, z, : rows - HALF]
 
 
-def gather_kernel(zs, own_ref, later_ref, note_ref, in_ref, out_ref, piece_ref, notes_ref, held, *sems):
+def normalise(steps, token_ref, gain_ref, normed_ref, s):
+    spans, quarters = token_ref.shape[:2]
+    share = spans * quarters // steps
+    for q in range(s * share, (s + 1) * share):
+        block = token_ref[q // quarters, q % quarters].astype(jnp.float32)
+        meansq = jnp.mean(block * block, axis=-1, keepdims=True)
+        made = block * lax.rsqrt(meansq + 1e-06) * gain_ref[...]
+        normed_ref[q // quarters, q % quarters] = made.astype(normed_ref.dtype)
+
+
+def gather_kernel(zs, own_ref, later_ref, note_ref, token_ref, gain_ref, in_ref, out_ref, piece_ref, notes_ref, normed_ref, held, *sems):
     moves = Gather(zs, own_ref, held, sems[:7])
     also = Ring(zs, later_ref, piece_ref, sems[8:10], sems[10])
     nsend, nrecv, nlocal = sems[11:]
@@ -227,7 +239,7 @@
     for i, to in enumerate(near):
         told.append(moves.copy(note_ref, notes_ref.at[g], nsend.at[i], nrecv.at[i], to))
         told[-1].start()
-    moves.run(sems[7], also)
+    moves.run(sems[7], also, functools.partial(normalise, zs // 2, token_ref, gain_ref, normed_ref))
     unpad(zs, held, (in_ref, out_ref))
     also.finish()
     keep.wait()
@@ -245,7 +257,16 @@
     )
 
 
-def sums_kernel(zs, piece_ref, part_ref, key_ref, value_ref, got_ref, held, relay, ysend, yrecv, xsend, xrecv, psend, precv, local):
+def encode(normed_ref, in_ref, out_ref, of):
+    spans, _, rows, width = normed_ref.shape
+    block = normed_ref[:, of].reshape(spans * rows, width)
+    pre = jnp.dot(block, in_ref[...], preferred_element_type=jnp.float32)
+    hidden = (0.5 * pre * (1.0 + lax.erf(pre * 0.5**0.5))).astype(block.dtype)
+    made = lax.dot_general(hidden, out_ref[...], (((1,), (1,)), ((), ())), preferred_element_type=jnp.float32)
+    return made.reshape(spans, rows, width)
+
+
+def sums_kernel(zs, piece_ref, normed_ref, token_ref, in_ref, out_ref, key_ref, value_ref, states_ref, held, part_ref, own_ref, got_ref, relay, ysend, yrecv, xsend, xrecv, psend, precv, local):
     core, x, z, m = ring_place()
     turn = 1 - 2 * core
     xf, xb, xo = (x + 4 + turn) % 4, (x + 4 - turn) % 4, (x + 2) % 4
@@ -267,8 +288,6 @@
         make(4, relay.at[0], got_ref.at[2, low], to_up),
         make(5, relay.at[1], got_ref.at[2, high], to_down),
     ]
-    for copy in copies[:4]:
-        copy.start()
     keep = pltpu.make_async_copy(piece_ref, held.at[x, core], local)
     keep.start()
     here = held.at[x, core]
@@ -279,6 +298,10 @@
     to_front.start()
     to_back.start()
     swaps = [remote(ref, ref, psend, precv, i, to_core) for i, ref in enumerate((here, back, front, over))]
+    for of, ready in ((far, copies[:2]), (up, copies[2:3]), (down, copies[3:4])):
+        part_ref[:, of] = encode(normed_ref, in_ref, out_ref, of).astype(part_ref.dtype)
+        for copy in ready:
+            copy.start()
     keep.wait()
     swaps[0].start()
     for i in range(2):
@@ -287,6 +310,7 @@
     remote(back, back, xsend, xrecv, 0, to_f).wait_recv()
     onward.start()
     swaps[1].start()
+    own_ref[...] = encode(normed_ref, in_ref, out_ref, m)
     remote(front, front, xsend, xrecv, 1, to_b).wait_recv()
     swaps[2].start()
     remote(over, over, xsend, xrecv, 2, to_f).wait_recv()
@@ -297,11 +321,16 @@
     unpad(zs, held, (key_ref, value_ref))
     for copy in copies[2:]:
         copy.wait_recv()
+    for j in range(states_ref.shape[0]):
+        total = own_ref[j]
+        for i in range(3):
+            total += got_ref[i, j].astype(jnp.float32)
+        states_ref[j] = (token_ref[j, m].astype(jnp.float32) + total).astype(states_ref.dtype)
     for copy in copies + [to_front, to_back, onward] + swaps:
         copy.wait_send()
 
 
-def route_kernel(owner_ref, count_ref, states_ref, key_ref, value_ref, query_ref, out_ref, send, cand, full_ref, keys, values, rsend, rrecv, ysend, yrecv, local):
+def route_kernel(note_ref, states_ref, key_ref, value_ref, query_ref, out_ref, send, cand, full_ref, keys, values, rsend, rrecv, ysend, yrecv, local):
     core, x, z, m = ring_place()
     g, d = lax.axis_index("grp"), lax.axis_index("dp")
     up, down, far = (m + 1) % 4, (m + 3) % 4, (m + 2) % 4
@@ -317,7 +346,7 @@
         apart = low_gap + jnp.where(core == source % 2, 0, 1)
         rank = jnp.int32(0)
         for i in range(spans):
-            target = owner_ref[source * spans + i]
+            target = note_ref[source, 0, i]
             leaves = (target < source * block) | (target >= (source + 1) * block)
             for r in range(2):
                 picks[r] = jnp.where(leaves & (rank == r) & (apart == 0), i, picks[r])
@@ -325,7 +354,7 @@
             for j in range(spans):
                 mine = target == (g * lax.axis_size("dp") + d) * spans + j
                 finds[j] = jnp.where(mine, spot, finds[j])
-                lives[j] = jnp.where(mine, count_ref[source * spans + i], lives[j])
+                lives[j] = jnp.where(mine, note_ref[source, 1, i], lives[j])
             rank = rank + jnp.where(leaves, 1, 0)
 
     for r in range(2):
@@ -453,7 +482,7 @@
     return pltpu.SemaphoreType.DMA(shape)
 
 
-def gather_first(first, second, later, note):
+def gather_first(first, second, later, note, tokens, gain):
     rows, width = first.shape
     zs = lax.axis_size("dp") // 2
     whole = jax.ShapeDtypeStruct((rows * zs * 2, width), first.dtype)
@@ -462,26 +491,36 @@
         whole,
         jax.ShapeDtypeStruct((zs,) + later.shape[2:], later.dtype),
         jax.ShapeDtypeStruct((4,) + note.shape, note.dtype),
+        jax.ShapeDtypeStruct(tokens.shape, tokens.dtype),
     ]
     one = pltpu.SemaphoreType.DMA
     scratch = [pltpu.VMEM((4, 2, zs, HALF, width), first.dtype)] + gather_sems(zs)
     scratch += [dma(2, zs // 2), dma(2, zs // 2), one, dma(3), dma(3), one]
     body = functools.partial(gather_kernel, zs)
-    return call(body, [pltpu.VMEM] * 3, outs, scratch, 0, "gather_first")(halves(first, second), later, note)
-
-
-def sum_over_units(parts, piece, features):
+    ins = (halves(first, second), later, note, tokens, gain)
+    return call(body, [pltpu.VMEM] * 5, outs, scratch, 0, "gather_first")(*ins)
+
+
+def encode_and_sum(piece, normed, tokens, full_in, full_out):
     zs = piece.shape[0]
-    spans, _, rows, width = parts.shape
-    whole = jax.ShapeDtypeStruct((features, piece.shape[2]), piece.dtype)
-    outs = [whole, whole, jax.ShapeDtypeStruct((3, spans, rows, width), parts.dtype)]
-    scratch = [pltpu.VMEM((4, 2) + piece.shape, piece.dtype), pltpu.VMEM((2, 2, rows, width), parts.dtype)]
+    spans, _, rows, width = tokens.shape
+    kind = tokens.dtype
+    whole = jax.ShapeDtypeStruct((width, piece.shape[2]), kind)
+    outs = [whole, whole, jax.ShapeDtypeStruct((spans, rows, width), kind)]
+    scratch = [
+        pltpu.VMEM((4, 2) + piece.shape, kind),
+        pltpu.VMEM(tokens.shape, kind),
+        pltpu.VMEM((spans, rows, width), jnp.float32),
+        pltpu.VMEM((3, spans, rows, width), kind),
+        pltpu.VMEM((2, 2, rows, width), kind),
+    ]
     scratch += [dma(6), dma(6), dma(3), dma(3), dma(4), dma(4), pltpu.SemaphoreType.DMA]
     body = functools.partial(sums_kernel, zs)
-    return call(body, [pltpu.VMEM] * 2, outs, scratch, 1, "sum_over_units")(piece, parts)
-
-
-def route_and_attend(owners, senders, states, key, value, queries):
+    ins = (piece, normed, tokens, full_in, full_out)
+    return call(body, [pltpu.VMEM] * 5, outs, scratch, 1, "encode_and_sum")(*ins)
+
+
+def route_and_attend(notes, states, key, value, queries):
     spans, rows, width = states.shape
     kind = states.dtype
     outs = [jax.ShapeDtypeStruct(queries.shape, kind)]
@@ -494,31 +533,19 @@
         held,
     ]
     scratch += [dma(3), dma(3), dma(6), dma(6), pltpu.SemaphoreType.DMA]
-    ins = [pltpu.SMEM] * 2 + [pltpu.VMEM] * 4
-    return call(route_kernel, ins, outs, scratch, 2, "route_and_attend")(owners, senders, states, key, value, queries)[0]
+    ins = [pltpu.SMEM] + [pltpu.VMEM] * 4
+    return call(route_kernel, ins, outs, scratch, 2, "route_and_attend")(notes, states, key, value, queries)[0]
 
 
 def on_device(neighbours, counts, owner, norm_gain, w_in, w_out, w_key, w_value, queries):
     span_count, key_len, enc_width = neighbours.shape
-    m = lax.axis_index("mp")
+    tokens = neighbours.reshape(span_count, 4, key_len // 4, enc_width)
     note = jnp.pad(jnp.stack([owner, counts]), ((0, 6), (0, 128 - span_count)))
-    full_in, full_out, piece, notes = gather_first(w_in, w_out.T, halves(w_key, w_value), note)
-    flat = neighbours.astype(jnp.float32).reshape(-1, enc_width)
-    meansq = jnp.mean(flat * flat, axis=-1, keepdims=True)
-    normed = (flat * lax.rsqrt(meansq + 1e-06) * norm_gain).astype(jnp.bfloat16)
-    pre = jnp.dot(normed, full_in, preferred_element_type=jnp.float32)
-    hidden = jax.nn.gelu(pre, approximate=False).astype(jnp.bfloat16)
-    partial_out = jnp.dot(hidden, full_out.T, preferred_element_type=jnp.float32)
-    parts = partial_out.astype(jnp.bfloat16).reshape(span_count, 4, key_len // 4, enc_width)
-    full_key, full_value, got = sum_over_units(parts, piece, enc_width)
-    own = lax.dynamic_index_in_dim(parts, m, 1, keepdims=False).astype(jnp.float32)
-    rows = neighbours.reshape(parts.shape)
-    rows = lax.dynamic_index_in_dim(rows, m, 1, keepdims=False).astype(jnp.float32)
-    got = got.astype(jnp.float32)
-    states = (rows + (own + got[0] + got[1] + got[2])).astype(jnp.bfloat16)
-    owners = notes[:, 0, :span_count].reshape(-1)
-    senders = notes[:, 1, :span_count].reshape(-1)
-    return route_and_attend(owners, senders, states, full_key, full_value, queries)
+    later = halves(w_key, w_value)
+    gain = norm_gain.reshape(1, enc_width)
+    full_in, full_out, piece, notes, normed = gather_first(w_in, w_out.T, later, note, tokens, gain)
+    full_key, full_value, states = encode_and_sum(piece, normed, tokens, full_in, full_out)
+    return route_and_attend(notes, states, full_key, full_value, queries)
 
 
 def solution(mesh):

time: 155 us -> 135 us (0.87)
  matrix products: 13.9 us -> 0 us
  other arithmetic: 12.1 us -> 3.73 us
  Pallas kernels: 124 us -> 127 us
    dot_general x1 -> x0, matrix products: 13.9 us -> none  [on_device(): jnp.dot(hidden, full_out.T, preferred_element_type=jnp.float32)]
    convert_element_type x3 -> x0, other arithmetic: 6.15 us -> none  [the longest x1 2.41 us: on_device(): normed = (flat * lax.rsqrt(meansq + 1e-06) * norm_gain).astype(jnp.bfloat16)]
    pallas_call x2, Pallas kernels: 82.8 us -> 85.1 us  [the longest x1 51.5 us: gather_first(): return call(body, [pltpu.VMEM] * 5, outs, scratch, 0, 'gather_first')(*ins)]
    reduce_sum x1 -> x0, other arithmetic: 2.05 us -> none  [on_device(): meansq = jnp.mean(flat * flat, axis=-1, keepdims=True)]
where the time goes in v4:
time: 135 us; the launch traced here: 134 us
  Pallas kernels  127 us (94%)
  local copies, waits for them, and re-layouts  3.74 us (3%)
  other arithmetic  3.73 us (3%)
    pallas_call x1, Pallas kernels, gather_first(): return call(body, [pltpu.VMEM] * 5, outs, scratch, 0, 'gather_first')(*ins)  51.5 us
    pallas_call x1, Pallas kernels, route_and_attend(): call(route_kernel, ins, outs, scratch, 2, 'route_and_attend')  41.6 us
    pallas_call x1, Pallas kernels, encode_and_sum(): call(body, [pltpu.VMEM] * 5, outs, scratch, 1, 'encode_and_sum')(*ins)  33.6 us
    another operation x2, other arithmetic, halves(): pair = jnp.stack([first, second])  3.05 us

profile of v4, /device:TPU:1, one launch (start us, length us, event | category | flops | bytes accessed | tf_op | source)
XLA Modules:
  0.0 134.2 jit_solution(172786730019527489)
XLA Ops:
  0.0 0.7 pad_add_fusion
  0.7 0.6 pad.14.note_ref
  1.3 1.3 reshape.15.gain_ref
  2.6 1.5 %fusion.5 = bf16[2,32,896]{2,1,0:T(8,128)(2,1)} fusion(bf16[1,28,896]{2,1,0:T(8,128)(2,1)} %bitcast.17, bf16[1,28,896]{2,1,0:T(8,128)(2,1)} %bitcast.18), kind=kLoop, calls=%fused_computation.7 | loop fusion | flops 401408 | bytes 215040 | tf_op jit(solution)/shard_map/stack | solution.py:464
  4.1 1.5 %fusion.4 = bf16[2,32,1024]{2,1,0:T(8,128)(2,1)} fusion(bf16[1,28,1024]{2,1,0:T(8,128)(2,1)} %bitcast.15, bf16[1,28,1024]{2,1,0:T(8,128)(2,1)} %bitcast.16), kind=kLoop, calls=%fused_computation.6 | loop fusion | flops 458752 | bytes 245760 | tf_op jit(solution)/shard_map/stack | solution.py:464
  5.6 51.5 %gather_first.1 = (bf16[896,896]{1,0:T(8,128)(2,1)}, bf16[896,896]{1,0:T(8,128)(2,1)}, bf16[16,16,1024]{2,1,0:T(8,128)(2,1)}, s32[4,8,128]{2,1,0:T(8,128)}, bf16[4,4,64,896]{3,2,1,0:T(8,128)(2,1)}) custom-call(bf16[2,2,16,896]{3,2,1,0:T(8,128)(2,1)} %bitcast.14, bf16[2,2,16,1024]{3,2,1,0:T(8,128)(2,1)} %bitcast.13, s32[8,128]{1,0:T(8,128)} %pad.14.note_ref, ...), custom_call_target="tpu_custom_call" | custom-call | tf_op jit(solution)/shard_map/gather_first/pallas_call | solution.py:501
  57.1 33.6 %encode_and_sum.1 = (bf16[896,1024]{1,0:T(8,128)(2,1)}, bf16[896,1024]{1,0:T(8,128)(2,1)}, bf16[4,64,896]{2,1,0:T(8,128)(2,1)}) custom-call(bf16[16,16,1024]{2,1,0:T(8,128)(2,1)} %get-tuple-element.14.piece_ref, bf16[4,4,64,896]{3,2,1,0:T(8,128)(2,1)} %get-tuple-element.15.normed_ref, bf16[4,4,64,896]{3,2,1,0:T(8,128)(2,1)} %bitcast.12, ...), custom_call_target="tpu_custom_call" | custom-call | tf_op jit(solution)/shard_map/encode_and_sum/pallas_call | solution.py:520
  90.7 41.6 %route_and_attend.1 = bf16[256,1024]{1,0:T(8,128)(2,1)} custom-call(s32[4,8,128]{2,1,0:T(8,128)} %get-tuple-element.13.note_ref, bf16[4,64,896]{2,1,0:T(8,128)(2,1)} %get-tuple-element.18.states_ref, bf16[896,1024]{1,0:T(8,128)(2,1)} %get-tuple-element.19.key_ref, bf16[896,1024]{1,0:T(8,128)(2,1)} %get-tuple-element.20.value_ref, bf16[256,1024]{1,0:T(8,128)(2,1)} %query_ref.1), custom_call_target="tpu_custom_call" | custom-call | tf_op jit(solution)/shard_map/route_and_attend/pallas_call | solution.py:537
  132.3 1.9 %copy.11 = bf16[256,1024]{1,0:T(8,128)(2,1)} copy(bf16[256,1024]{1,0:T(8,128)(2,1)} %route_and_attend.1) | data formatting | bytes 1048576

commit v5 on v4

--- a/solution.py
+++ b/solution.py
@@ -216,11 +216,32 @@
     for q in range(s * share, (s + 1) * share):
         block = token_ref[q // quarters, q % quarters].astype(jnp.float32)
         meansq = jnp.mean(block * block, axis=-1, keepdims=True)
-        made = block * lax.rsqrt(meansq + 1e-06) * gain_ref[...]
+        made = block * lax.rsqrt(meansq + 1e-06) * gain_ref[...].reshape(1, -1)
         normed_ref[q // quarters, q % quarters] = made.astype(normed_ref.dtype)
 
 
-def gather_kernel(zs, own_ref, later_ref, note_ref, token_ref, gain_ref, in_ref, out_ref, piece_ref, notes_ref, normed_ref, held, *sems):
+def lay_out(half_ref, weights):
+    for a, weight in enumerate(weights):
+        rest = weight.shape[0] - HALF
+        half_ref[a, 0] = weight[:HALF]
+        half_ref[a, 1, :rest] = weight[HALF:]
+        half_ref[a, 1, rest:] = jnp.zeros((HALF - rest, weight.shape[1]), weight.dtype)
+
+
+def write_note(note_ref, lists):
+    row = lax.broadcasted_iota(jnp.int32, note_ref.shape, 0)
+    lane = lax.broadcasted_iota(jnp.int32, note_ref.shape, 1)
+    made = jnp.zeros(note_ref.shape, jnp.int32)
+    for k, values in enumerate(lists):
+        for i in range(values.shape[0]):
+            made = jnp.where((row == k) & (lane == i), values[i], made)
+    note_ref[...] = made
+
+
+def gather_kernel(zs, owner_ref, count_ref, win_ref, wout_ref, wkey_ref, wvalue_ref, token_ref, gain_ref, in_ref, out_ref, piece_ref, notes_ref, normed_ref, held, own_ref, later_ref, note_ref, *sems):
+    lay_out(own_ref, (win_ref, wout_ref))
+    lay_out(later_ref, (wkey_ref, wvalue_ref))
+    write_note(note_ref, (owner_ref, count_ref))
     moves = Gather(zs, own_ref, held, sems[:7])
     also = Ring(zs, later_ref, piece_ref, sems[8:10], sems[10])
     nsend, nrecv, nlocal = sems[11:]
@@ -460,12 +481,6 @@
     lax.fori_loop(0, width // HEAD, head, 0)
 
 
-def halves(first, second):
-    pair = jnp.stack([first, second])
-    pad = jnp.pad(pair, ((0, 0), (0, 2 * HALF - first.shape[0]), (0, 0)))
-    return pad.reshape(2, 2, HALF, first.shape[1])
-
-
 def call(body, ins, outs, scratch, collective_id, name):
     return pl.pallas_call(
         body,
@@ -482,23 +497,29 @@
     return pltpu.SemaphoreType.DMA(shape)
 
 
-def gather_first(first, second, later, note, tokens, gain):
+def gather_first(owner, counts, first, second, key, value, tokens, gain):
     rows, width = first.shape
     zs = lax.axis_size("dp") // 2
-    whole = jax.ShapeDtypeStruct((rows * zs * 2, width), first.dtype)
+    kind = first.dtype
+    whole = jax.ShapeDtypeStruct((rows * zs * 2, width), kind)
     outs = [
         whole,
         whole,
-        jax.ShapeDtypeStruct((zs,) + later.shape[2:], later.dtype),
-        jax.ShapeDtypeStruct((4,) + note.shape, note.dtype),
+        jax.ShapeDtypeStruct((zs, HALF, key.shape[1]), kind),
+        jax.ShapeDtypeStruct((4, 8, 128), jnp.int32),
         jax.ShapeDtypeStruct(tokens.shape, tokens.dtype),
     ]
     one = pltpu.SemaphoreType.DMA
-    scratch = [pltpu.VMEM((4, 2, zs, HALF, width), first.dtype)] + gather_sems(zs)
-    scratch += [dma(2, zs // 2), dma(2, zs // 2), one, dma(3), dma(3), one]
+    scratch = [
+        pltpu.VMEM((4, 2, zs, HALF, width), kind),
+        pltpu.VMEM((2, 2, HALF, width), kind),
+        pltpu.VMEM((2, 2, HALF, key.shape[1]), kind),
+        pltpu.VMEM((8, 128), jnp.int32),
+    ]
+    scratch += gather_sems(zs) + [dma(2, zs // 2), dma(2, zs // 2), one, dma(3), dma(3), one]
     body = functools.partial(gather_kernel, zs)
-    ins = (halves(first, second), later, note, tokens, gain)
-    return call(body, [pltpu.VMEM] * 5, outs, scratch, 0, "gather_first")(*ins)
+    ins = (owner, counts, first, second, key, value, tokens, gain)
+    return call(body, [pltpu.SMEM] * 2 + [pltpu.VMEM] * 6, outs, scratch, 0, "gather_first")(*ins)
 
 
 def encode_and_sum(piece, normed, tokens, full_in, full_out):
@@ -540,10 +561,9 @@
 def on_device(neighbours, counts, owner, norm_gain, w_in, w_out, w_key, w_value, queries):
     span_count, key_len, enc_width = neighbours.shape
     tokens = neighbours.reshape(span_count, 4, key_len // 4, enc_width)
-    note = jnp.pad(jnp.stack([owner, counts]), ((0, 6), (0, 128 - span_count)))
-    later = halves(w_key, w_value)
-    gain = norm_gain.reshape(1, enc_width)
-    full_in, full_out, piece, notes, normed = gather_first(w_in, w_out.T, later, note, tokens, gain)
+    full_in, full_out, piece, notes, normed = gather_first(
+        owner, counts, w_in, w_out.T, w_key, w_value, tokens, norm_gain
+    )
     full_key, full_value, states = encode_and_sum(piece, normed, tokens, full_in, full_out)
     return route_and_attend(notes, states, full_key, full_value, queries)
 

time: 135 us -> 129 us (0.956)
  other arithmetic: 3.73 us -> 0 us
  local copies, waits for them, and re-layouts: 3.74 us -> 1.87 us
    another operation x3 -> x0, other arithmetic: 3.73 us -> none  [the longest x2 3.05 us: halves(): pair = jnp.stack([first, second])]
where the time goes in v5:
time: 129 us
  Pallas kernels  127 us (98%)
  local copies, waits for them, and re-layouts  1.87 us (1%)
    pallas_call x1, Pallas kernels, gather_first(): call(body, [pltpu.SMEM] * 2 + [pltpu.VMEM] * 6, outs, scratch, 0, 'gather...  51.9 us
    pallas_call x1, Pallas kernels, route_and_attend(): call(route_kernel, ins, outs, scratch, 2, 'route_and_attend')  41.7 us
    pallas_call x1, Pallas kernels, encode_and_sum(): call(body, [pltpu.VMEM] * 5, outs, scratch, 1, 'encode_and_sum')(*ins)  33.4 us

profile of v5, /device:TPU:1, one launch (start us, length us, event | category | flops | bytes accessed | tf_op | source)
XLA Modules:
  0.0 128.9 jit_solution(13199650922424118352)
XLA Ops:
  0.0 51.9 %gather_first.1 = (bf16[896,896]{1,0:T(8,128)(2,1)}, bf16[896,896]{1,0:T(8,128)(2,1)}, bf16[16,16,1024]{2,1,0:T(8,128)(2,1)}, s32[4,8,128]{2,1,0:T(8,128)}, bf16[4,4,64,896]{3,2,1,0:T(8,128)(2,1)}) custom-call(s32[4]{0:T(128)} %owner_ref.1, s32[4]{0:T(128)} %count_ref.1, bf16[28,896]{1,0:T(8,128)(2,1)} %win_ref.1, bf16[28,896]{1,0:T(8,128)(2,1)} %bitcast.4, ...), custom_call_target="tpu_custom_call" | custom-call | tf_op jit(solution)/shard_map/gather_first/pallas_call | solution.py:522
  51.9 33.4 %encode_and_sum.1 = (bf16[896,1024]{1,0:T(8,128)(2,1)}, bf16[896,1024]{1,0:T(8,128)(2,1)}, bf16[4,64,896]{2,1,0:T(8,128)(2,1)}) custom-call(bf16[16,16,1024]{2,1,0:T(8,128)(2,1)} %get-tuple-element.14.piece_ref, bf16[4,4,64,896]{3,2,1,0:T(8,128)(2,1)} %get-tuple-element.15.normed_ref, bf16[4,4,64,896]{3,2,1,0:T(8,128)(2,1)} %bitcast.3, ...), custom_call_target="tpu_custom_call" | custom-call | tf_op jit(solution)/shard_map/encode_and_sum/pallas_call | solution.py:541
  85.3 41.7 %route_and_attend.1 = bf16[256,1024]{1,0:T(8,128)(2,1)} custom-call(s32[4,8,128]{2,1,0:T(8,128)} %get-tuple-element.13.note_ref, bf16[4,64,896]{2,1,0:T(8,128)(2,1)} %get-tuple-element.18.states_ref, bf16[896,1024]{1,0:T(8,128)(2,1)} %get-tuple-element.19.key_ref, bf16[896,1024]{1,0:T(8,128)(2,1)} %get-tuple-element.20.value_ref, bf16[256,1024]{1,0:T(8,128)(2,1)} %query_ref.1), custom_call_target="tpu_custom_call" | custom-call | tf_op jit(solution)/shard_map/route_and_attend/pallas_call | solution.py:558
  127.0 1.9 %copy.11 = bf16[256,1024]{1,0:T(8,128)(2,1)} copy(bf16[256,1024]{1,0:T(8,128)(2,1)} %route_and_attend.1) | data formatting | bytes 1048576
